TPU v7x, 128 devices: a whole 4x4x4 slice. The times are simulated.
128 devices in a mesh: dp: 32 (over y, x, core), expert: 4 (over z).
Axes of the slice: x: 4, y: 4, z: 4, core: 2. Of those that a mesh axis runs over, the one named last changes fastest.
Arguments:
- tokens: bfloat16 [8192, 1024], P(('dp', 'expert')), may hold values from -6 to 6
- expert_ids: int32 [8192, 2], P(('dp', 'expert')), may hold values from 0 to 7, all different within a row; in each aligned block of 64 rows (0 to 63, 64 to 127, ...) at most 20 rows name the same one
- gate_weights: float32 [8192, 2], P(('dp', 'expert')), may hold values from 0.2 to 1
- w_gate: bfloat16 [8, 1024, 4096], P('expert', None, 'dp'), may hold values from -0.1875 to 0.1875
- w_up: bfloat16 [8, 1024, 4096], P('expert', None, 'dp'), may hold values from -0.1875 to 0.1875
- w_down: bfloat16 [8, 4096, 1024], P('expert', 'dp'), may hold values from -0.09375 to 0.09375
- cotangent: bfloat16 [8192, 1024], P(('dp', 'expert')), may hold values from -6 to 6
Outputs:
- mixed: bfloat16 [8192, 1024], P(('dp', 'expert'))
- grad_tokens: bfloat16 [8192, 1024], P(('dp', 'expert'))
- grad_gate: bfloat16 [8, 1024, 4096], P('expert', None, 'dp')
- grad_up: bfloat16 [8, 1024, 4096], P('expert', None, 'dp')
- grad_down: bfloat16 [8, 4096, 1024], P('expert', 'dp')
Inputs may be any that keep to these rules, and one draw needn't show every extreme that they name: `expert_ids`: in every aligned block of 64 rows (the rows of one device) no expert is named more than 20 times, a bound that some block reaches; the 2 experts of a row differ.
All inputs are finite; a program needn't handle non-finite values.
Results may differ from a plain program's by a relative error of at most 0.019.
Values may be sent and summed in bfloat16 or wider, within the bound.
A program may use at most 192 MiB of HBM per device.

v0:
```python
import jax
import jax.numpy as jnp
from jax import lax
from jax.sharding import PartitionSpec as P


def spread_one(buffer):
    arrived = lax.all_to_all(buffer, "expert", split_axis=0, concat_axis=0, tiled=True)
    return lax.all_gather(arrived[None], "dp", axis=0, tiled=True)


def collect(term_fn):
    summed = lax.psum_scatter(
        term_fn(jnp.int32(0), 1 * lax.axis_size("dp")).astype(jnp.bfloat16),
        "dp",
        scatter_dimension=0,
        tiled=True,
    )
    return lax.all_to_all(summed, "expert", split_axis=1, concat_axis=1, tiled=True)


def body(tokens, expert_ids, gate_weights, w_gate, w_up, w_down, cotangent):
    owners = lax.axis_size("expert")
    tok_count = tokens.shape[0]
    width = tokens.shape[1]
    top_count = expert_ids.shape[1]
    exp_local = w_gate.shape[0]
    experts_all = exp_local * owners
    capacity = max(2, 5 * tok_count * top_count // (4 * experts_all))
    flat = expert_ids.reshape(-1)
    onehot = (flat[:, None] == jnp.arange(experts_all, dtype=jnp.int32)[None, :]).astype(jnp.int32)
    before = jnp.sum((jnp.cumsum(onehot, axis=0) - onehot) * onehot, axis=1)
    slot = flat * capacity + before
    placer = (jnp.arange(experts_all * capacity, dtype=jnp.int32)[:, None] == slot[None, :]).astype(
        jnp.bfloat16
    )

    def place(rows):
        buffer = jnp.dot(placer, rows, preferred_element_type=jnp.float32).astype(jnp.bfloat16)
        return buffer.reshape(owners, exp_local, capacity, width)

    def unpack(results):
        flat_out = results.reshape(experts_all * capacity, width)
        return (
            jnp.take(flat_out, slot, axis=0)
            .astype(jnp.float32)
            .reshape(tok_count, top_count, width)
        )

    rows_x = jnp.repeat(tokens, top_count, axis=0)
    buf_x = place(rows_x)
    rows_d = (gate_weights[:, :, None] * cotangent[:, None, :].astype(jnp.float32)).reshape(
        tok_count * top_count, width
    )
    buf_d = place(rows_d.astype(jnp.bfloat16))
    gathered = spread_one(buf_x)
    gate = jnp.einsum("pcjkd,jdf->pcjkf", gathered, w_gate, preferred_element_type=jnp.float32)
    up = jnp.einsum("pcjkd,jdf->pcjkf", gathered, w_up, preferred_element_type=jnp.float32)
    sig = jax.nn.sigmoid(gate)
    act = gate * sig
    hidden = (act * up).astype(jnp.bfloat16)

    def forward_term(start, count):
        return jnp.einsum("pcjkf,jfd->pcjkd", hidden, w_down, preferred_element_type=jnp.float32)

    expert_out = collect(forward_term)
    mixed = jnp.sum(gate_weights[:, :, None] * unpack(expert_out), axis=1).astype(jnp.bfloat16)
    grad_rows = spread_one(buf_d)
    dact = jnp.einsum("pcjkd,jfd->pcjkf", grad_rows, w_down, preferred_element_type=jnp.float32)
    grad_hg = (dact * up * sig * (1.0 + gate * (1.0 - sig))).astype(jnp.bfloat16)
    grad_hu = (dact * act).astype(jnp.bfloat16)
    grad_down = jnp.einsum(
        "pcjkf,pcjkd->jfd", hidden, grad_rows, preferred_element_type=jnp.float32
    ).astype(jnp.bfloat16)
    grad_gate = jnp.einsum(
        "pcjkd,pcjkf->jdf", gathered, grad_hg, preferred_element_type=jnp.float32
    ).astype(jnp.bfloat16)
    grad_up = jnp.einsum(
        "pcjkd,pcjkf->jdf", gathered, grad_hu, preferred_element_type=jnp.float32
    ).astype(jnp.bfloat16)

    def backward_term(start, count):
        total = jnp.einsum("pcjkf,jdf->pcjkd", grad_hg, w_gate, preferred_element_type=jnp.float32)
        return total + jnp.einsum(
            "pcjkf,jdf->pcjkd", grad_hu, w_up, preferred_element_type=jnp.float32
        )

    token_part = collect(backward_term)
    grad_tokens = jnp.sum(unpack(token_part), axis=1).astype(jnp.bfloat16)
    return (mixed, grad_tokens, grad_gate, grad_up, grad_down)


def solution(mesh):
    placed = (
        P(("dp", "expert"), None),
        P(("dp", "expert"), None),
        P(("dp", "expert"), None),
        P("expert", None, "dp"),
        P("expert", None, "dp"),
        P("expert", "dp", None),
        P(("dp", "expert"), None),
    )
    return jax.shard_map(
        body,
        mesh=mesh,
        in_specs=placed,
        out_specs=(
            P(("dp", "expert"), None),
            P(("dp", "expert"), None),
            P("expert", None, "dp"),
            P("expert", None, "dp"),
            P("expert", "dp", None),
        ),
        check_vma=False,
    )
```

profile of v0, /device:TPU:1, one launch (start us, length us, event | category | flops | bytes accessed | tf_op | source)
XLA Modules:
  0.0 464.2 jit_solution(14023050609205363421)
XLA Ops:
  7.3 0.8 copy.29
  8.1 0.1 reshape.60
  8.2 0.1 fusion.51
  8.3 0.2 reduce_window_sum.11
  8.5 0.2 select_reduce_fusion
  8.7 1.0 broadcast_in_dim.24
  9.7 0.1 reshape.61
  9.8 0.2 convolution_convert_fusion.1
  10.2 0.3 copy.30
  10.5 12.0 %all_to_all.20 = bf16[4,2,20,1024]{3,1,2,0:T(2,128)(2,1)} all-to-all(bf16[4,2,20,1024]{3,1,2,0:T(2,128)(2,1)S(1)} %copy.30), channel_id=1, replica_groups=mesh['dp'=32,'expert'=4] {'expert'}, dimensions={0} | all-to-all | bytes 655360 | tf_op jit(solution)/shard_map/all_to_all | solution.py:8
  22.6 0.1 copy.28
  22.7 0.1 mul.67
  22.8 0.1 mul.69
  23.0 0.4 mul.70
  23.3 0.3 convolution_convert_fusion
  23.7 0.3 copy.37
  24.1 9.0 %all_to_all.21 = bf16[4,2,20,1024]{3,1,2,0:T(2,128)(2,1)} all-to-all(bf16[4,2,20,1024]{3,1,2,0:T(2,128)(2,1)S(1)} %copy.37), channel_id=1, replica_groups=mesh['dp'=32,'expert'=4] {'expert'}, dimensions={0} | all-to-all | bytes 655360 | tf_op jit(solution)/shard_map/all_to_all | solution.py:8
  33.0 0.6 all-reduce.5.cloned.1.call-start
  33.6 47.9 %all-gather.5.cloned.1.call-done = bf16[128,2,20,1024]{3,1,2,0:T(2,128)(2,1)} async-done(((bf16[4,2,20,1024]{3,1,2,0:T(2,128)(2,1)}), bf16[128,2,20,1024]{3,1,2,0:T(2,128)(2,1)}) %all-gather.5.cloned.1.call-update) | async-done | bytes 10485776 | tf_op jit(solution)/shard_map/all_gather | solution.py:9
  81.6 11.8 %fusion.9 = f32[2,32,4,20,128]{4,1,3,2,0:T(8,128)} fusion(bf16[32,4,2,20,1024]{4,2,3,1,0:T(2,128)(2,1)} %bitcast.92, bf16[2,1024,128]{2,1,0:T(8,128)(2,1)S(1)} %copy-done.6), kind=kOutput, calls=%fused_computation.13 | convolution fusion | flops 1342177280 | bytes 13631488 | tf_op jit(solution)/shard_map/pcjkd,jdf->pcjkf/dot_general | solution.py:58
  93.4 8.1 %fusion.11 = f32[2,32,4,20,128]{4,1,3,2,0:T(8,128)} fusion(bf16[32,4,2,20,1024]{4,2,3,1,0:T(2,128)(2,1)S(1)} %bitcast.95, bf16[2,1024,128]{2,1,0:T(8,128)(2,1)S(1)} %copy-done.4), kind=kOutput, calls=%fused_computation.15 | convolution fusion | flops 1342177280 | bytes 13631488 | tf_op jit(solution)/shard_map/pcjkd,jdf->pcjkf/dot_general | solution.py:57
  101.5 39.5 %all-gather.7.cloned.1.call-done = bf16[128,2,20,1024]{3,1,2,0:T(2,128)(2,1)} async-done(((bf16[4,2,20,1024]{3,1,2,0:T(2,128)(2,1)}), bf16[128,2,20,1024]{3,1,2,0:T(2,128)(2,1)}) %all-gather.7.cloned.1.call-update) | async-done | bytes 10485776 | tf_op jit(solution)/shard_map/all_gather | solution.py:9
  141.0 12.7 %fusion.16 = (bf16[32,4,2,20,128]{4,0,3,1,2:T(8,128)(2,1)S(1)}, bf16[32,4,2,20,128]{4,0,3,1,2:T(8,128)(2,1)S(1)}, bf16[32,4,2,20,128]{4,0,3,1,2:T(8,128)(2,1)S(1)}) fusion(f32[2,32,4,20,128]{4,1,3,2,0:T(8,128)} %fusion.11, f32[2,32,4,20,128]{4,1,3,2,0:T(8,128)} %fusion.9, bf16[2,128,1024]{2,1,0:T(8,128)(2,1)S(1)} %copy-done, ...), kind=kOutput, calls=%fused_computation.22 | convolution fusion | flops 1352007680 | bytes 20185088 | tf_op jit(solution)/shard_map/pcjkd,jfd->pcjkf/dot_general | solution.py:69
  153.7 3.3 convert_bitcast_fusion
  157.0 23.6 %copy.33 = bf16[32,4,2,20,1024]{4,1,3,2,0:T(4,128)(2,1)} copy(bf16[32,4,2,20,1024]{4,0,3,1,2:T(8,128)(2,1)S(1)} %convert_bitcast_fusion) | data formatting | bytes 20971520 | tf_op jit(solution)/shard_map/convert_element_type | solution.py:14
  180.6 8.5 %fusion.45 = f32[2,32,4,20,1024]{4,1,3,2,0:T(8,128)} fusion(bf16[32,4,2,20,128]{4,0,3,1,2:T(8,128)(2,1)S(1)} %get-tuple-element.11, bf16[2,1024,128]{2,1,0:T(8,128)(2,1)S(1)} %copy-done.5), kind=kOutput, calls=%fused_computation.43 | convolution fusion | flops 1342177280 | bytes 22806528 | tf_op jit(solution)/shard_map/pcjkf,jdf->pcjkd/dot_general | solution.py:83
  189.1 12.4 %fusion = bf16[32,4,2,20,1024]{4,0,3,1,2:T(8,128)(2,1)} fusion(f32[2,32,4,20,1024]{4,1,3,2,0:T(8,128)} %fusion.45, bf16[32,4,2,20,128]{4,0,3,1,2:T(8,128)(2,1)S(1)} %get-tuple-element.10, bf16[2,1024,128]{2,1,0:T(8,128)(2,1)} %param.13), kind=kOutput, calls=%fused_computation.3 | convolution fusion | flops 1352663040 | bytes 33292288 | tf_op jit(solution)/shard_map/pcjkf,jdf->pcjkd/dot_general | solution.py:84
  201.6 15.1 %copy.39 = bf16[32,4,2,20,1024]{4,1,3,2,0:T(4,128)(2,1)} copy(bf16[32,4,2,20,1024]{4,0,3,1,2:T(8,128)(2,1)} %fusion) | data formatting | bytes 20971520 | tf_op jit(solution)/shard_map/convert_element_type | solution.py:14
  216.7 0.6 copy-done.10
  217.3 0.6 dynamic-slice
  217.9 17.8 %fusion.37 = bf16[2,1024,128]{2,1,0:T(8,128)(2,1)} fusion(bf16[32,4,2,20,128]{4,0,3,1,2:T(8,128)(2,1)S(1)} %get-tuple-element.10, bf16[32,4,2,20,1024]{4,2,3,1,0:T(2,128)(2,1)} %bitcast.93), kind=kOutput, calls=%fused_computation.37 | convolution fusion | flops 1342439424 | bytes 12320768 | tf_op jit(solution)/shard_map/pcjkd,pcjkf->jdf/dot_general | solution.py:78
  235.8 167.7 %all-reduce.5.cloned.1.call-done = (bf16[32,4,2,20,1024]{4,1,3,2,0:T(4,128)(2,1)}, bf16[32,4,2,20,1024]{4,1,3,2,0:T(4,128)(2,1)}) async-done(((bf16[32,4,2,20,1024]{4,1,3,2,0:T(4,128)(2,1)}, bf16[32,4,2,20,1024]{4,1,3,2,0:T(4,128)(2,1)}), (bf16[32,4,2,20,1024]{4,1,3,2,0:T(4,128)(2,1)}, bf16[32,4,2,20,1024]{4,1,3,2,0:T(4,128)(2,1)})) %all-reduce.5.cloned.1.call-update) | async-done | bytes 20971536
  403.5 1.7 constant_dynamic-slice_fusion
  405.2 1.1 copy.40
  406.3 4.1 all-to-all-start.3
  410.4 18.0 %fusion.40 = bf16[2,1024,128]{2,1,0:T(8,128)(2,1)} fusion(bf16[32,4,2,20,128]{4,0,3,1,2:T(8,128)(2,1)S(1)} %get-tuple-element.11, bf16[32,4,2,20,1024]{4,2,3,1,0:T(2,128)(2,1)} %bitcast.94), kind=kOutput, calls=%fused_computation.38 | convolution fusion | flops 1342439424 | bytes 12320768 | tf_op jit(solution)/shard_map/pcjkd,pcjkf->jdf/dot_general | solution.py:75
  428.4 1.7 constant_dynamic-slice_fusion.1
  430.1 1.1 copy.34
  431.2 4.2 all-to-all-start.1
  435.4 16.4 %fusion.32 = bf16[2,128,1024]{2,1,0:T(8,128)(2,1)} fusion(bf16[32,4,2,20,1024]{4,2,3,1,0:T(2,128)(2,1)} %bitcast.97, bf16[32,4,2,20,128]{4,0,3,1,2:T(8,128)(2,1)S(1)} %copy-done.3), kind=kOutput, calls=%fused_computation.36 | convolution fusion | flops 1342439424 | bytes 12320768 | tf_op jit(solution)/shard_map/pcjkf,pcjkd->jfd/dot_general | solution.py:72
  452.0 0.1 copy.35
  452.2 1.1 gather_fusion.1
  453.3 0.9 gather_fusion
  454.1 0.1 broadcast_select_fusion
  454.3 0.1 reshape.68
  454.4 0.3 reshape.71
  454.7 1.4 multiply_reduce_fusion
  456.1 1.3 reduce
  (36 shorter events, 0.6 us)
Async XLA Ops:
  7.2 133.8 %copy-start = (bf16[2,128,1024]{2,1,0:T(8,128)(2,1)S(1)}, bf16[2,128,1024]{2,1,0:T(8,128)(2,1)}, u32[]{:S(2)}) copy-start(bf16[2,128,1024]{2,1,0:T(8,128)(2,1)} %param.14) | copy-start | bytes 1572868
  7.2 15.4 %copy-start.8 = (f32[64,2]{0,1:T(2,128)S(1)}, f32[64,2]{0,1:T(2,128)}, u32[]{:S(2)}) copy-start(f32[64,2]{0,1:T(2,128)} %param.11) | copy-start | bytes 1540
  7.2 15.6 %copy-start.7 = (bf16[64,1024]{1,0:T(8,128)(2,1)S(1)}, bf16[64,1024]{1,0:T(8,128)(2,1)}, u32[]{:S(2)}) copy-start(bf16[64,1024]{1,0:T(8,128)(2,1)} %param.15) | copy-start | bytes 393220
  7.2 74.4 %all-gather.5.cloned.1.call-start = ((), (), s32[]{:S(2)}) async-start(), calls=%async_computation.4 | async-start | bytes 10813440 | tf_op jit(solution)/shard_map/all_gather | solution.py:9
  22.5 59.1 %copy-start.6 = (bf16[2,1024,128]{2,1,0:T(8,128)(2,1)S(1)}, bf16[2,1024,128]{2,1,0:T(8,128)(2,1)}, u32[]{:S(2)}) copy-start(bf16[2,1024,128]{2,1,0:T(8,128)(2,1)} %param.13) | copy-start | bytes 1572868
  22.5 118.5 %all-gather.7.cloned.1.call-start = ((), (), s32[]{:S(2)}) async-start(), calls=%async_computation.5 | async-start | bytes 10813440 | tf_op jit(solution)/shard_map/all_gather | solution.py:9
  33.0 370.4 %all-reduce.5.cloned.1.call-start = ((), (), s32[]{:S(2)}) async-start(), calls=%async_computation.6 | async-start | bytes 41943040
  81.6 11.8 %copy-start.4 = (bf16[2,1024,128]{2,1,0:T(8,128)(2,1)S(1)}, bf16[2,1024,128]{2,1,0:T(8,128)(2,1)}, u32[]{:S(2)}) copy-start(bf16[2,1024,128]{2,1,0:T(8,128)(2,1)} %param.12) | copy-start | bytes 1572868
  81.6 11.8 %copy-start.9 = (bf16[128,2,20,1024]{3,1,2,0:T(2,128)(2,1)S(1)}, bf16[128,2,20,1024]{3,1,2,0:T(2,128)(2,1)}, u32[]{:S(2)}) copy-start(bf16[128,2,20,1024]{3,1,2,0:T(2,128)(2,1)} %all-gather.5.cloned.1.call-done) | copy-start | bytes 31457284
  153.7 3.3 copy-start.2
  157.0 23.6 %copy-start.5 = (bf16[2,1024,128]{2,1,0:T(8,128)(2,1)S(1)}, bf16[2,1024,128]{2,1,0:T(8,128)(2,1)}, u32[]{:S(2)}) copy-start(bf16[2,1024,128]{2,1,0:T(8,128)(2,1)} %param.12) | copy-start | bytes 1572868
  216.7 0.7 copy-start.10
  406.3 24.9 %all-to-all-start.3 = ((bf16[1,4,2,20,1024]{4,2,3,0,1:T(2,128)(2,1)}), bf16[1,4,2,20,1024]{4,2,3,0,1:T(2,128)(2,1)S(1)}, u32[]{:S(2)}, u32[]{:S(2)}) async-start(bf16[1,4,2,20,1024]{4,2,3,0,1:T(2,128)(2,1)} %copy.40), calls=%async_computation.3 | async-start | bytes 655360 | tf_op jit(solution)/shard_map/all_to_all | solution.py:19
  410.4 25.0 %copy-start.3 = (bf16[32,4,2,20,128]{4,0,3,1,2:T(8,128)(2,1)S(1)}, bf16[32,4,2,20,128]{4,0,3,1,2:T(8,128)(2,1)}, u32[]{:S(2)}) copy-start(bf16[32,4,2,20,128]{4,0,3,1,2:T(8,128)(2,1)} %copy-done.2) | copy-start | bytes 3932164
  431.2 20.8 %all-to-all-start.1 = ((bf16[1,4,2,20,1024]{4,2,3,0,1:T(2,128)(2,1)}), bf16[1,4,2,20,1024]{4,2,3,0,1:T(2,128)(2,1)S(1)}, u32[]{:S(2)}, u32[]{:S(2)}) async-start(bf16[1,4,2,20,1024]{4,2,3,0,1:T(2,128)(2,1)} %copy.34), calls=%async_computation.1 | async-start | bytes 655360 | tf_op jit(solution)/shard_map/all_to_all | solution.py:19
  452.1 5.2 %copy-start.1 = (bf16[2,128,1024]{2,1,0:T(8,128)(2,1)S(1)}, bf16[2,128,1024]{2,1,0:T(8,128)(2,1)}, u32[]{:S(2)}) copy-start(bf16[2,128,1024]{2,1,0:T(8,128)(2,1)} %param.14) | copy-start | bytes 1572868
Sparse Core Ops, SparseCore 0:
  22.6 58.8 all-gather.4
  83.8 57.1 all-gather.6
  216.8 186.5 all-reduce.4
where the time goes:
time: 469 us; the launch traced here: 464 us
  waiting for transfers between devices  255 us (54%)
  matrix products  110 us (23%)
  local copies, waits for them, and re-layouts  51.9 us (11%)
  blocking collectives  20.9 us (4%)
  between operations  14.3 us (3%)
  starting transfers between devices  9.02 us (2%)
    unnamed x4, waiting for transfers between devices  168 us
    all_gather x2, waiting for transfers between devices, spread_one(): return lax.all_gather(arrived[None], 'dp', axis=0, tiled=True)  87.5 us
    convert_element_type x2, local copies, waits for them, and re-layouts, collect(): term_fn(jnp.int32(0), 1 * lax.axis_size('dp')).astype(jnp.bfloat16)  38.7 us
    all_to_all x2, blocking collectives, spread_one(): lax.all_to_all(buffer, 'expert', split_axis=0, concat_axis=0, tiled=True)  20.9 us
    dot_general x1, matrix products, body(): jnp.einsum('pcjkd,pcjkf->jdf', gathered, grad_hg, preferred_element_type=...  18 us
    dot_general x1, matrix products, body(): jnp.einsum('pcjkd,pcjkf->jdf', gathered, grad_hu, preferred_element_type=...  17.8 us
    dot_general x1, matrix products, body(): jnp.einsum('pcjkf,pcjkd->jfd', hidden, grad_rows, preferred_element_type=...  16.4 us
    dot_general x1, matrix products, body(): jnp.einsum('pcjkd,jfd->pcjkf', grad_rows, w_down, preferred_element_type=...  12.7 us
  transfers between devices with their start and end apart: 5, of which 3 were waited for; matrix products, arithmetic and copies ran while one was open for 17% of the time, Pallas kernels for 0%

commit v1 on v0

v1 whole, which is shorter than its diff:
```python
import jax
import jax.numpy as jnp
from jax import lax
from jax.sharding import PartitionSpec as P


def body(tokens, expert_ids, gate_weights, w_gate, w_up, w_down, cotangent):
    owners = lax.axis_size("expert")
    n_dp = lax.axis_size("dp")
    tok_count, width = tokens.shape
    top_count = expert_ids.shape[1]
    exp_local = w_gate.shape[0]
    experts_all = exp_local * owners
    capacity = max(2, 5 * tok_count * top_count // (4 * experts_all))
    same_core = [list(range(c, n_dp, 2)) for c in range(2)]
    swap = [(i, i ^ 1) for i in range(n_dp)]

    flat = expert_ids.reshape(-1)
    onehot = (flat[:, None] == jnp.arange(experts_all, dtype=jnp.int32)[None, :]).astype(jnp.int32)
    before = jnp.sum((jnp.cumsum(onehot, axis=0) - onehot) * onehot, axis=1)
    slot = flat * capacity + before
    placer = (jnp.arange(experts_all * capacity, dtype=jnp.int32)[:, None] == slot[None, :]).astype(
        jnp.bfloat16
    )

    def place(rows):
        buffer = jnp.dot(placer, rows, preferred_element_type=jnp.float32).astype(jnp.bfloat16)
        return buffer.reshape(owners, exp_local, capacity, width)

    def spread(buffer):
        arrived = lax.all_to_all(buffer, "expert", split_axis=0, concat_axis=0, tiled=True)
        arrived = arrived.transpose(1, 0, 2, 3).reshape(exp_local, owners * capacity, width)
        return lax.all_gather(arrived, "dp", axis=0, tiled=False, axis_index_groups=same_core)

    def collect(partial):
        summed = lax.psum_scatter(
            partial, "dp", scatter_dimension=0, tiled=False, axis_index_groups=same_core
        )
        summed = summed.reshape(exp_local, owners, capacity, width).transpose(1, 0, 2, 3)
        return lax.all_to_all(summed, "expert", split_axis=0, concat_axis=0, tiled=True)

    def unpack(results):
        flat_out = results.reshape(experts_all * capacity, width)
        picked = lax.dot_general(
            placer, flat_out, (((0,), (0,)), ((), ())), preferred_element_type=jnp.float32
        )
        return picked.reshape(tok_count, top_count, width)

    def other(v):
        return lax.ppermute(v, "dp", swap)

    wg2, wu2, wd2 = other(w_gate), other(w_up), other(w_down)
    wg = jnp.concatenate([w_gate, wg2], axis=2)
    wu = jnp.concatenate([w_up, wu2], axis=2)
    wd = jnp.concatenate([w_down, wd2], axis=1)
    half = w_gate.shape[2]

    buf_x = place(jnp.repeat(tokens, top_count, axis=0))
    rows_d = (gate_weights[:, :, None] * cotangent[:, None, :].astype(jnp.float32)).reshape(
        tok_count * top_count, width
    )
    buf_d = place(rows_d.astype(jnp.bfloat16))
    xs = spread(buf_x)
    gate = jnp.einsum("pjcd,jdf->pjcf", xs, wg, preferred_element_type=jnp.float32)
    up = jnp.einsum("pjcd,jdf->pjcf", xs, wu, preferred_element_type=jnp.float32)
    sig = jax.nn.sigmoid(gate)
    act = gate * sig
    hidden = (act * up).astype(jnp.bfloat16)
    part_o = jnp.einsum("pjcf,jfd->pjcd", hidden, wd, preferred_element_type=jnp.float32)
    out_rows = collect(part_o.astype(jnp.bfloat16))
    mixed = jnp.sum(gate_weights[:, :, None] * unpack(out_rows), axis=1).astype(jnp.bfloat16)

    ds = spread(buf_d)
    dact = jnp.einsum("pjcd,jfd->pjcf", ds, wd, preferred_element_type=jnp.float32)
    dg = (dact * up * sig * (1.0 + gate * (1.0 - sig))).astype(jnp.bfloat16)
    du = (dact * act).astype(jnp.bfloat16)
    part_v = jnp.einsum("pjcf,jdf->pjcd", dg, wg, preferred_element_type=jnp.float32)
    part_v = part_v + jnp.einsum("pjcf,jdf->pjcd", du, wu, preferred_element_type=jnp.float32)
    grad_tokens = jnp.sum(unpack(collect(part_v.astype(jnp.bfloat16))), axis=1).astype(jnp.bfloat16)

    gd = jnp.einsum("pjcf,pjcd->jfd", hidden, ds, preferred_element_type=jnp.float32)
    gg = jnp.einsum("pjcd,pjcf->jdf", xs, dg, preferred_element_type=jnp.float32)
    gu = jnp.einsum("pjcd,pjcf->jdf", xs, du, preferred_element_type=jnp.float32)

    def total(mine, theirs):
        arrived = other(theirs.astype(jnp.bfloat16))
        return (mine + arrived.astype(jnp.float32)).astype(jnp.bfloat16)

    grad_down = total(gd[:, :half], gd[:, half:])
    grad_gate = total(gg[:, :, :half], gg[:, :, half:])
    grad_up = total(gu[:, :, :half], gu[:, :, half:])
    return (mixed, grad_tokens, grad_gate, grad_up, grad_down)


def solution(mesh):
    rows = P(("dp", "expert"), None)
    cols = P("expert", None, "dp")
    down = P("expert", "dp", None)
    return jax.shard_map(
        body,
        mesh=mesh,
        in_specs=(rows, rows, rows, cols, cols, down, rows),
        out_specs=(rows, rows, cols, cols, down),
        check_vma=False,
    )
```

time: 469 us -> 349 us (0.74)
  matrix products: 110 us -> 41.8 us
  local copies, waits for them, and re-layouts: 51.9 us -> 14.4 us
  waiting for transfers between devices: 255 us -> 236 us
    dot_general x9 -> x11, matrix products: 109 us -> 41.3 us  [the longest x1 7.12 us: body(): jnp.einsum('pjcd,jfd->pjcf', ds, wd, preferred_element_type=jnp.float32)]
    convert_element_type x2 -> x0, local copies, waits for them, and re-layouts: 38.7 us -> none  [collect(): term_fn(jnp.int32(0), 1 * lax.axis_size('dp')).astype(jnp.bfloat16)]
    unnamed x4, waiting for transfers between devices: 168 us -> 139 us
    all_to_all x2, waiting for transfers between devices: 0.01 us -> 6.25 us  [collect(): lax.all_to_all(summed, 'expert', split_axis=0, concat_axis=0, tiled=True)]
    ppermute x0 -> x6, starting transfers between devices: none -> 5.57 us  [other(): return lax.ppermute(v, 'dp', swap)]
    convert_element_type x0 -> x3, other arithmetic: none -> 5.17 us  [total(): return (mine + arrived.astype(jnp.float32)).astype(jnp.bfloat16)]
  transfers between devices with their start and end apart: 5 -> 11, of which waited for: 3 -> 6; matrix products, arithmetic and copies ran while one was open for 17% -> 10% of each run, Pallas kernels for 0% -> 0%
where the time goes in v1:
time: 349 us; the launch traced here: 345 us
  waiting for transfers between devices  236 us (68%)
  matrix products  41.8 us (12%)
  blocking collectives  20.1 us (6%)
  local copies, waits for them, and re-layouts  14.4 us (4%)
  between operations  14.2 us (4%)
  starting transfers between devices  13.3 us (4%)
  other arithmetic  5.69 us (2%)
    unnamed x4, waiting for transfers between devices  139 us
    all_gather x2, waiting for transfers between devices, spread(): lax.all_gather(arrived, 'dp', axis=0, tiled=False, axis_index_groups=same...  89.8 us
    all_to_all x2, blocking collectives, spread(): lax.all_to_all(buffer, 'expert', split_axis=0, concat_axis=0, tiled=True)  20.1 us
    all_to_all x2, starting transfers between devices, collect(): lax.all_to_all(summed, 'expert', split_axis=0, concat_axis=0, tiled=True)  7.59 us
    dot_general x1, matrix products, body(): jnp.einsum('pjcd,jfd->pjcf', ds, wd, preferred_element_type=jnp.float32)  7.12 us
  transfers between devices with their start and end apart: 11, of which 6 were waited for; matrix products, arithmetic and copies ran while one was open for 10% of the time, Pallas kernels for 0%

profile of v1, /device:TPU:1, one launch (start us, length us, event | category | flops | bytes accessed | tf_op | source)
XLA Modules:
  0.0 345.3 jit_solution(5812251243802954115)
XLA Ops:
  7.2 0.8 copy.30
  8.3 0.2 reduce_window_sum.11
  8.4 0.2 select_reduce_fusion
  8.6 1.0 broadcast_in_dim.2
  9.8 0.2 convolution_convert_fusion.1
  10.1 0.3 copy.31
  10.5 11.9 %all_to_all.20 = bf16[4,2,20,1024]{3,1,2,0:T(2,128)(2,1)S(1)} all-to-all(bf16[4,2,20,1024]{3,1,2,0:T(2,128)(2,1)S(1)} %copy.31), channel_id=1, replica_groups=mesh['dp'=32,'expert'=4] {'expert'}, dimensions={0} | all-to-all | bytes 655360 | tf_op jit(solution)/shard_map/all_to_all | solution.py:31
  22.3 0.8 copy.32
  23.6 0.4 mul.70
  24.0 0.3 convolution_convert_fusion
  24.4 0.3 copy.37
  24.7 8.3 %all_to_all.21 = bf16[4,2,20,1024]{3,1,2,0:T(2,128)(2,1)S(1)} all-to-all(bf16[4,2,20,1024]{3,1,2,0:T(2,128)(2,1)S(1)} %copy.37), channel_id=1, replica_groups=mesh['dp'=32,'expert'=4] {'expert'}, dimensions={0} | all-to-all | bytes 655360 | tf_op jit(solution)/shard_map/all_to_all | solution.py:31
  33.0 0.8 copy.38
  33.9 3.3 collective-permute-start.2
  37.3 0.4 collective-permute-start
  37.7 1.0 collective-permute-done.2
  38.7 41.4 %all-gather.3.cloned.1.call-done = bf16[16,2,80,1024]{3,2,0,1:T(8,128)(2,1)} async-done(((bf16[1,2,80,1024]{3,2,0,1:T(8,128)(2,1)}), bf16[16,2,80,1024]{3,2,0,1:T(8,128)(2,1)}) %all-gather.3.cloned.1.call-update) | async-done | bytes 5242896 | tf_op jit(solution)/shard_map/all_gather | solution.py:33
  80.2 5.8 %fusion.15 = f32[2,256,16,80]{1,3,2,0:T(8,128)} fusion(bf16[16,2,80,1024]{3,2,0,1:T(8,128)(2,1)} %all-gather.3.cloned.1.call-done, bf16[2,1024,128]{2,1,0:T(8,128)(2,1)S(1)} %collective-permute-done.2, bf16[2,1024,128]{2,1,0:T(8,128)(2,1)S(1)} %copy-done.3), kind=kOutput, calls=%fused_computation.39 | convolution fusion | flops 1344274432 | bytes 8912896 | tf_op jit(solution)/shard_map/pjcd,jdf->pjcf/dot_general | solution.py:65
  85.9 3.0 fusion.16
  89.0 0.8 copy-done.14
  89.8 48.3 %all-gather.5.cloned.1.call-done = bf16[16,2,80,1024]{3,2,0,1:T(8,128)(2,1)} async-done(((bf16[1,2,80,1024]{3,2,0,1:T(8,128)(2,1)}), bf16[16,2,80,1024]{3,2,0,1:T(8,128)(2,1)}) %all-gather.5.cloned.1.call-update) | async-done | bytes 5242896 | tf_op jit(solution)/shard_map/all_gather | solution.py:33
  138.1 7.1 %fusion.3 = (bf16[16,2,80,256]{3,2,0,1:T(8,128)(2,1)S(1)}, bf16[16,2,80,256]{3,2,0,1:T(8,128)(2,1)S(1)}, bf16[16,2,80,256]{3,2,0,1:T(8,128)(2,1)S(1)}) fusion(f32[2,256,16,80]{1,3,2,0:T(8,128)} %fusion.15, f32[2,256,16,80]{1,3,2,0:T(8,128)} %fusion.16, bf16[16,2,80,1024]{3,2,0,1:T(8,128)(2,1)} %all-gather.5.cloned.1.call-done, ...), kind=kOutput, calls=%fused_computation.7 | convolution fusion | flops 1354104832 | bytes 15466496 | tf_op jit(solution)/shard_map/pjcd,jfd->pjcf/dot_general | solution.py:74
  145.3 5.4 %convert_bitcast_fusion = bf16[16,2,80,1024]{3,2,0,1:T(8,128)(2,1)} fusion(bf16[16,2,80,256]{3,2,0,1:T(8,128)(2,1)S(1)} %get-tuple-element.8, bf16[2,128,1024]{2,1,0:T(8,128)(2,1)S(1)} %copy-done.15, bf16[2,128,1024]{2,1,0:T(8,128)(2,1)} %param.12), kind=kOutput, calls=%fused_computation.2 | convolution fusion | flops 1346895872 | bytes 7602176 | tf_op jit(solution)/shard_map/pjcf,jfd->pjcd/dot_general | solution.py:69
  150.7 1.6 fusion.14
  152.3 4.0 %fusion = bf16[16,2,80,1024]{3,2,0,1:T(8,128)(2,1)} fusion(f32[2,1024,16,80]{1,3,2,0:T(8,128)S(1)} %fusion.14, bf16[16,2,80,256]{3,2,0,1:T(8,128)(2,1)S(1)} %get-tuple-element.7, bf16[2,1024,128]{2,1,0:T(8,128)(2,1)S(1)} %copy-done.9, bf16[2,1024,128]{2,1,0:T(8,128)(2,1)S(1)} %copy-done.5), kind=kOutput, calls=%fused_computation.1 | convolution fusion | flops 1349517312 | bytes 18087936 | tf_op jit(solution)/shard_map/pjcf,jdf->pjcd/dot_general | solution.py:77
  156.5 0.5 copy-done.16
  157.0 0.6 dynamic-slice
  157.6 4.5 %convolution_bitcast_fusion = f32[2,256,1024]{2,1,0:T(8,128)S(1)} fusion(bf16[16,2,80,256]{3,2,0,1:T(8,128)(2,1)} %copy-done.17, bf16[16,2,80,1024]{3,2,0,1:T(8,128)(2,1)} %all-gather.5.cloned.1.call-done), kind=kOutput, calls=%fused_computation.18 | convolution fusion | flops 1342177280 | bytes 8650752 | tf_op jit(solution)/shard_map/pjcf,pjcd->jfd/dot_general | solution.py:81
  162.1 1.2 collective-permute-start.5
  163.3 5.9 %convolution_bitcast_fusion.2 = f32[2,1024,256]{2,1,0:T(8,128)S(1)} fusion(bf16[16,2,80,1024]{3,2,0,1:T(8,128)(2,1)} %all-gather.3.cloned.1.call-done, bf16[16,2,80,256]{3,2,0,1:T(8,128)(2,1)S(1)} %get-tuple-element.7), kind=kOutput, calls=%fused_computation.20 | convolution fusion | flops 1342177280 | bytes 8650752 | tf_op jit(solution)/shard_map/pjcd,pjcf->jdf/dot_general | solution.py:82
  169.2 1.0 slice.47
  170.2 0.5 copy-done.2
  170.7 2.2 convolution_bitcast_fusion.1
  173.0 1.3 copy-done
  174.4 0.6 collective-permute-start.4
  175.0 0.9 fusion.11
  175.9 138.8 %all-reduce.5.cloned.1.call-done = (bf16[16,2,80,1024]{3,2,0,1:T(8,128)(2,1)}, bf16[16,2,80,1024]{3,2,0,1:T(8,128)(2,1)}) async-done(((bf16[16,2,80,1024]{3,2,0,1:T(8,128)(2,1)}, bf16[16,2,80,1024]{3,2,0,1:T(8,128)(2,1)}), (bf16[16,2,80,1024]{3,2,0,1:T(8,128)(2,1)}, bf16[16,2,80,1024]{3,2,0,1:T(8,128)(2,1)})) %all-reduce.5.cloned.1.call-update) | async-done | bytes 10485776
  314.7 1.8 constant_dynamic-slice_fusion
  316.5 1.1 copy.39
  317.6 4.1 %all-to-all-start.3 = ((bf16[4,2,20,1024]{3,1,2,0:T(2,128)(2,1)}), bf16[4,2,20,1024]{3,1,2,0:T(2,128)(2,1)S(1)}, u32[]{:S(2)}, u32[]{:S(2)}) async-start(bf16[4,2,20,1024]{3,1,2,0:T(2,128)(2,1)} %bitcast.21), calls=%async_computation.3 | async-start | bytes 655360 | tf_op jit(solution)/shard_map/all_to_all | solution.py:40
  321.7 2.3 fusion.13
  324.0 1.1 copy.33
  325.0 2.5 all-to-all-done.3
  327.6 3.5 all-to-all-start.1
  331.1 2.0 fusion.12
  333.2 3.7 %all-to-all-done.1 = bf16[4,2,20,1024]{3,1,2,0:T(2,128)(2,1)S(1)} async-done(((bf16[4,2,20,1024]{3,1,2,0:T(2,128)(2,1)}), bf16[4,2,20,1024]{3,1,2,0:T(2,128)(2,1)S(1)}, u32[]{:S(2)}, u32[]{:S(2)}) %all-to-all-start.1) | async-done | bytes 327712 | tf_op jit(solution)/shard_map/all_to_all | solution.py:40
  337.0 0.9 convolution_reduce_fusion
  337.9 0.9 fusion.10
  (67 shorter events, 1.8 us)
Async XLA Ops:
  7.2 16.0 %copy-start.11 = (f32[64,2]{0,1:T(2,128)S(1)}, f32[64,2]{0,1:T(2,128)}, u32[]{:S(2)}) copy-start(f32[64,2]{0,1:T(2,128)} %param.9) | copy-start | bytes 1540
  7.2 16.3 %copy-start.10 = (bf16[64,1024]{1,0:T(8,128)(2,1)S(1)}, bf16[64,1024]{1,0:T(8,128)(2,1)}, u32[]{:S(2)}) copy-start(bf16[64,1024]{1,0:T(8,128)(2,1)} %param.13) | copy-start | bytes 393220
  7.2 73.0 %all-gather.3.cloned.1.call-start = ((), (), s32[]{:S(2)}) async-start(), calls=%async_computation.4 | async-start | bytes 5570560 | tf_op jit(solution)/shard_map/all_gather | solution.py:33
  23.1 115.0 %all-gather.5.cloned.1.call-start = ((), (), s32[]{:S(2)}) async-start(), calls=%async_computation.5 | async-start | bytes 5570560 | tf_op jit(solution)/shard_map/all_gather | solution.py:33
  23.6 10.3 %copy-start.3 = (bf16[2,1024,128]{2,1,0:T(8,128)(2,1)S(1)}, bf16[2,1024,128]{2,1,0:T(8,128)(2,1)}, u32[]{:S(2)}) copy-start(bf16[2,1024,128]{2,1,0:T(8,128)(2,1)} %param.11) | copy-start | bytes 1572868
  23.6 13.6 %copy-start.4 = (bf16[2,1024,128]{2,1,0:T(8,128)(2,1)S(1)}, bf16[2,1024,128]{2,1,0:T(8,128)(2,1)}, u32[]{:S(2)}) copy-start(bf16[2,1024,128]{2,1,0:T(8,128)(2,1)} %param.10) | copy-start | bytes 1572868
  23.6 13.7 %copy-start.13 = (bf16[2,128,1024]{2,1,0:T(8,128)(2,1)S(1)}, bf16[2,128,1024]{2,1,0:T(8,128)(2,1)}, u32[]{:S(2)}) copy-start(bf16[2,128,1024]{2,1,0:T(8,128)(2,1)} %param.12) | copy-start | bytes 1572868
  33.8 280.9 %all-reduce.5.cloned.1.call-start = ((), (), s32[]{:S(2)}) async-start(), calls=%async_computation.6 | async-start | bytes 20971520
  33.9 4.9 %collective-permute-start.2 = (bf16[2,1024,128]{2,1,0:T(8,128)(2,1)S(1)}, bf16[2,1024,128]{2,1,0:T(8,128)(2,1)S(1)}, u32[]{:S(2)}, u32[]{:S(2)}) collective-permute-start(bf16[2,1024,128]{2,1,0:T(8,128)(2,1)S(1)} %copy-done.3), channel_id=1, source_target_pairs={{0,4},{4,0},{8,12},{12,8},{16,20},{20,16},{24,28},{28,24},{32,36},... | collective-permute-start | bytes 1572872 | tf_op jit(solution)/shard_map/ppermute | solution.py:50
  37.2 48.7 %collective-permute-start.1 = (bf16[2,1024,128]{2,1,0:T(8,128)(2,1)S(1)}, bf16[2,1024,128]{2,1,0:T(8,128)(2,1)S(1)}, u32[]{:S(2)}, u32[]{:S(2)}) collective-permute-start(bf16[2,1024,128]{2,1,0:T(8,128)(2,1)S(1)} %copy-done.4), channel_id=1, source_target_pairs={{0,4},{4,0},{8,12},{12,8},{16,20},{20,16},{24,28},{28,24},{32,36},... | collective-permute-start | bytes 1572872 | tf_op jit(solution)/shard_map/ppermute | solution.py:50
  37.3 51.7 %collective-permute-start = (bf16[2,128,1024]{2,1,0:T(8,128)(2,1)S(1)}, bf16[2,128,1024]{2,1,0:T(8,128)(2,1)S(1)}, u32[]{:S(2)}, u32[]{:S(2)}) collective-permute-start(bf16[2,128,1024]{2,1,0:T(8,128)(2,1)S(1)} %copy-done.13), channel_id=1, source_target_pairs={{0,4},{4,0},{8,12},{12,8},{16,20},{20,16},{24,28},{28,24},{32,36},... | collective-permute-start | bytes 1572872 | tf_op jit(solution)/shard_map/ppermute | solution.py:50
  38.7 47.2 %copy-start.6 = (bf16[2,1024,128]{2,1,0:T(8,128)(2,1)}, bf16[2,1024,128]{2,1,0:T(8,128)(2,1)S(1)}, u32[]{:S(2)}) copy-start(bf16[2,1024,128]{2,1,0:T(8,128)(2,1)S(1)} %collective-permute-done.2) | copy-start | bytes 1572868
  80.2 5.8 %copy-start.12 = (bf16[16,2,80,1024]{3,2,0,1:T(8,128)(2,1)S(1)}, bf16[16,2,80,1024]{3,2,0,1:T(8,128)(2,1)}, u32[]{:S(2)}) copy-start(bf16[16,2,80,1024]{3,2,0,1:T(8,128)(2,1)} %all-gather.3.cloned.1.call-done) | copy-start | bytes 15728644
  85.9 3.1 copy-start.8
  89.0 0.8 copy-start.14
  138.1 7.1 %copy-start.15 = (bf16[2,128,1024]{2,1,0:T(8,128)(2,1)S(1)}, bf16[2,128,1024]{2,1,0:T(8,128)(2,1)}, u32[]{:S(2)}) copy-start(bf16[2,128,1024]{2,1,0:T(8,128)(2,1)} %copy-done.14) | copy-start | bytes 1572868
  145.3 5.4 %copy-start.17 = (bf16[16,2,80,256]{3,2,0,1:T(8,128)(2,1)}, bf16[16,2,80,256]{3,2,0,1:T(8,128)(2,1)S(1)}, u32[]{:S(2)}) copy-start(bf16[16,2,80,256]{3,2,0,1:T(8,128)(2,1)S(1)} %get-tuple-element.8) | copy-start | bytes 3932164
  145.3 5.4 %copy-start.7 = (bf16[2,1024,128]{2,1,0:T(8,128)(2,1)S(1)}, bf16[2,1024,128]{2,1,0:T(8,128)(2,1)}, u32[]{:S(2)}) copy-start(bf16[2,1024,128]{2,1,0:T(8,128)(2,1)} %copy-done.6) | copy-start | bytes 1572868
  150.7 1.6 copy-start.5
  150.7 1.6 copy-start.9
  156.3 0.7 copy-start.16
  162.0 8.7 %slice-start = ((s8[5242880]{0:T(1024)(128)(4,1)}), s8[4194304]{0:T(1024)(128)(4,1)S(1)}, s32[]{:S(2)}) async-start(s8[5242880]{0:T(1024)(128)(4,1)} %bitcast.113), calls=%async_computation.7 | async-start | bytes 8388608
  162.1 8.6 %slice-start.1 = ((s8[5242880]{0:T(1024)(128)(4,1)}), s8[1048576]{0:T(1024)(128)(4,1)S(1)}, s32[]{:S(2)}) async-start(s8[5242880]{0:T(1024)(128)(4,1)} %bitcast.113), calls=%async_computation.8 | async-start | bytes 2097152
  162.1 12.9 %collective-permute-start.5 = (bf16[2,128,1024]{2,1,0:T(8,128)(2,1)S(1)}, bf16[2,128,1024]{2,1,0:T(8,128)(2,1)S(1)}, u32[]{:S(2)}, u32[]{:S(2)}) collective-permute-start(bf16[2,128,1024]{2,1,0:T(8,128)(2,1)S(1)} %slice.45), channel_id=1, source_target_pairs={{0,4},{4,0},{8,12},{12,8},{16,20},{20,16},{24,28},{28,24},{32,36},... | collective-permute-start | bytes 1572872 | tf_op jit(solution)/shard_map/ppermute | solution.py:50
  169.2 1.5 copy-start.2
  170.7 151.0 %collective-permute-start.3 = (bf16[2,1024,128]{2,1,0:T(8,128)(2,1)}, bf16[2,1024,128]{2,1,0:T(8,128)(2,1)}, u32[]{:S(2)}, u32[]{:S(2)}) collective-permute-start(bf16[2,1024,128]{2,1,0:T(8,128)(2,1)} %slice.47), channel_id=1, source_target_pairs={{0,4},{4,0},{8,12},{12,8},{16,20},{20,16},{24,28},{28,24},{32,36},... | collective-permute-start | bytes 1572872 | tf_op jit(solution)/shard_map/ppermute | solution.py:50
  173.0 1.4 copy-start
  174.4 156.7 %collective-permute-start.4 = (bf16[2,1024,128]{2,1,0:T(8,128)(2,1)S(1)}, bf16[2,1024,128]{2,1,0:T(8,128)(2,1)}, u32[]{:S(2)}, u32[]{:S(2)}) collective-permute-start(bf16[2,1024,128]{2,1,0:T(8,128)(2,1)S(1)} %slice.46), channel_id=1, source_target_pairs={{0,4},{4,0},{8,12},{12,8},{16,20},{20,16},{24,28},{28,24},{32,36},... | collective-permute-start | bytes 1572872 | tf_op jit(solution)/shard_map/ppermute | solution.py:50
  316.5 14.6 %copy-start.1 = (f32[2,1024,256]{2,1,0:T(8,128)S(1)}, f32[2,1024,256]{2,1,0:T(8,128)}, u32[]{:S(2)}) copy-start(f32[2,1024,256]{2,1,0:T(8,128)} %copy-done) | copy-start | bytes 6291460
  317.6 10.0 %all-to-all-start.3 = ((bf16[4,2,20,1024]{3,1,2,0:T(2,128)(2,1)}), bf16[4,2,20,1024]{3,1,2,0:T(2,128)(2,1)S(1)}, u32[]{:S(2)}, u32[]{:S(2)}) async-start(bf16[4,2,20,1024]{3,1,2,0:T(2,128)(2,1)} %bitcast.21), calls=%async_computation.3 | async-start | bytes 655360 | tf_op jit(solution)/shard_map/all_to_all | solution.py:40
  327.6 9.3 %all-to-all-start.1 = ((bf16[4,2,20,1024]{3,1,2,0:T(2,128)(2,1)}), bf16[4,2,20,1024]{3,1,2,0:T(2,128)(2,1)S(1)}, u32[]{:S(2)}, u32[]{:S(2)}) async-start(bf16[4,2,20,1024]{3,1,2,0:T(2,128)(2,1)} %bitcast.12), calls=%async_computation.1 | async-start | bytes 655360 | tf_op jit(solution)/shard_map/all_to_all | solution.py:40
Sparse Core Ops, SparseCore 0:
  23.3 56.8 all-gather.2
  82.3 55.7 all-gather.4
  156.5 158.1 all-reduce.4

commit v2 on v1

v2 whole, which is shorter than its diff:
```python
import jax
import jax.numpy as jnp
from jax import lax
from jax.experimental import pallas as pl
from jax.experimental.pallas import tpu as pltpu
from jax.sharding import PartitionSpec as P

MESH = pl.DeviceIdType.MESH
BF, F32 = jnp.bfloat16, jnp.float32
TOK, D, CAP = 64, 1024, 20
PLANES, EXP = 4, 2
SLAB = 48
ALL = PLANES * SLAB
ROWS = PLANES * CAP
SLOTS = 8
MINE = SLOTS * ROWS
HALF = D // 2
FP = 128
HID = 4 * FP
COPIES = 128


def dot(a, b, contract=(1, 0)):
    return lax.dot_general(a, b, (((contract[0],), (contract[1],)), ((), ())), preferred_element_type=F32)


class Net:
    def __init__(self, send, recv):
        self.send, self.recv, self.all = send, recv, []

    def go(self, src, dst, device):
        k = len(self.all)
        copy = pltpu.make_async_remote_copy(
            src_ref=src, dst_ref=dst, send_sem=self.send.at[k], recv_sem=self.recv.at[k],
            device_id=device, device_id_type=MESH,
        )
        copy.start()
        self.all.append(copy)
        return copy


def got(*copies):
    for copy in copies:
        copy.wait_recv()


def left(ref, e, s):
    return ref.at[e, s, :, pl.ds(0, HALF)]


def right(ref, e, s):
    return ref.at[e, s, :, pl.ds(HALF, HALF)]


class Gather:
    def __init__(self, net, ref, xp, yu, yd):
        self.net, self.ref, self.xp, self.yu, self.yd = net, ref, xp, yu, yd

    def start(self):
        go, g = self.net.go, self.ref
        self.x0 = go(g.at[0, 0], g.at[0, 4], self.xp)
        self.u1 = go(g.at[1, 0], g.at[1, 3], self.yu)
        self.d1 = go(g.at[1, 0], g.at[1, 1], self.yd)
        self.u00 = go(g.at[0, 0], g.at[0, 3], self.yu)
        self.d00 = go(g.at[0, 0], g.at[0, 1], self.yd)
        self.x1 = [go(g.at[1, 0], g.at[1, 4], self.xp)]

    def step2(self):
        go, g = self.net.go, self.ref
        got(self.x0)
        self.u01 = go(g.at[0, 4], g.at[0, 7], self.yu)
        self.d01 = go(g.at[0, 4], g.at[0, 5], self.yd)
        got(self.u1)
        self.fu1 = go(left(g, 1, 3), left(g, 1, 2), self.yu)
        self.x1.append(go(g.at[1, 3], g.at[1, 7], self.xp))
        got(self.d1)
        self.fd1 = go(right(g, 1, 1), right(g, 1, 2), self.yd)
        self.x1.append(go(g.at[1, 1], g.at[1, 5], self.xp))
        got(self.u00)
        self.fu00 = go(left(g, 0, 3), left(g, 0, 2), self.yu)
        got(self.d00)
        self.fd00 = go(right(g, 0, 1), right(g, 0, 2), self.yd)

    def step3(self):
        go, g = self.net.go, self.ref
        got(self.u01)
        self.fu01 = go(left(g, 0, 7), left(g, 0, 6), self.yu)
        got(self.d01)
        self.fd01 = go(right(g, 0, 5), right(g, 0, 6), self.yd)
        got(self.fu1, self.fd1)
        self.x1.append(go(g.at[1, 2], g.at[1, 6], self.xp))

    def finish(self, e):
        if e == 0:
            got(self.fu00, self.fd00, self.fu01, self.fd01)
        else:
            got(*self.x1)


def add_half(p, e, s, lo, arrived):
    cols = pl.ds(lo, HALF)
    p[e, s, :, cols] = (p[e, s, :, cols].astype(F32) + arrived[...].astype(F32)).astype(BF)


class Reduce:
    def __init__(self, net, part, near, far, across, xp, yu, yd):
        self.net, self.p, self.near, self.far, self.across = net, part, near, far, across
        self.xp, self.yu, self.yd = xp, yu, yd
        self.ring = {}

    def outer(self, key, e, b):
        go, p = self.net.go, self.p
        self.ring[key] = [
            go(left(p, e, b + 2), self.near.at[key, 0], self.yu),
            go(right(p, e, b + 2), self.near.at[key, 1], self.yd),
        ]

    def free_up(self, key, e, b):
        self.ring[key].append(self.net.go(right(self.p, e, b + 1), right(self.far, key, 0), self.yu))

    def free_down(self, key, e, b):
        self.ring[key].append(self.net.go(left(self.p, e, b + 3), left(self.far, key, 1), self.yd))

    def inner(self, key, e, b):
        go, p = self.net.go, self.p
        got(self.ring[key][0])
        add_half(p, e, b + 1, 0, self.near.at[key, 0])
        up = go(left(p, e, b + 1), left(self.far, key, 0), self.yu)
        got(self.ring[key][1])
        add_half(p, e, b + 3, HALF, self.near.at[key, 1])
        down = go(right(p, e, b + 3), right(self.far, key, 1), self.yd)
        self.ring[key] += [up, down]

    def total(self, key, e, b):
        got(*self.ring[key][2:])
        return self.p[e, b].astype(F32) + self.far[key, 0].astype(F32) + self.far[key, 1].astype(F32)

    def start0(self):
        for dx in (1, 0):
            self.outer(dx, 0, 4 * dx)
        for dx in (1, 0):
            self.free_up(dx, 0, 4 * dx)
            self.free_down(dx, 0, 4 * dx)

    def start1(self):
        self.x1 = {dy: self.net.go(self.p.at[1, 4 + dy], self.across.at[dy], self.xp) for dy in (2, 1, 3, 0)}

    def joined(self, dy):
        got(self.x1[dy])
        self.p[1, dy] = (self.p[1, dy].astype(F32) + self.across[dy].astype(F32)).astype(BF)

    def step2(self):
        self.joined(2)
        self.outer(2, 1, 0)
        self.inner(1, 0, 4)
        self.inner(0, 0, 0)
        self.joined(1)
        self.free_up(2, 1, 0)
        self.joined(3)
        self.free_down(2, 1, 0)
        self.joined(0)

    def step3(self):
        self.p[0, 4] = self.total(1, 0, 4).astype(BF)
        self.x0 = self.net.go(self.p.at[0, 4], self.across.at[4], self.xp)
        self.inner(2, 1, 0)

    def step4(self):
        rows0 = self.total(0, 0, 0)
        got(self.x0)
        rows0 = (rows0 + self.across[4].astype(F32)).astype(BF)
        rows1 = self.total(2, 1, 0).astype(BF)
        return jnp.concatenate([rows0, rows1], axis=0)


def kernel(
    tok, ids, gw, cot, wg, wu, wd,
    mixed, gtok, ggate, gup, gdown,
    send_x, send_d, arr_x, arr_d, send_o, send_v, arr_o, arr_v,
    xg, dg, po, pv, near_o, far_o, across_o, near_v, far_v, across_v,
    wgu, wdn, fac_a, fac_b, hid, dgu, pd, pgu, rd, rgu, rd2, rgu2,
    send, recv, local,
):
    dp, z = lax.axis_index("dp"), lax.axis_index("expert")
    core, x, y = dp % 2, (dp // 2) % 4, dp // 8

    def at(yy, xx, cc):
        return ((yy * 4 + xx) * 2 + cc, z)

    xp = at(y, x + 1 - 2 * (x % 2), core)
    xc = at(y, 3 - x, core)
    yu, yd = at((y + 1) % 4, x, core), at((y + 3) % 4, x, core)
    cp = at(y, x, 1 - core)
    zs = {r: (dp, (z + r) % 4) for r in (1, 2, 3)}

    barrier = pltpu.get_barrier_semaphore()
    for device in (xp, xc, yu, yd, cp, zs[1], zs[2], zs[3]):
        pl.semaphore_signal(barrier, inc=1, device_id=device, device_id_type=MESH)

    own = [
        pltpu.make_async_copy(wg, wgu.at[:, :, pl.ds(0, FP)], local.at[0]),
        pltpu.make_async_copy(wu, wgu.at[:, :, pl.ds(HID, FP)], local.at[1]),
        pltpu.make_async_copy(wd, wdn.at[:, pl.ds(0, FP), :], local.at[2]),
    ]
    for copy in own:
        copy.start()

    lane = lax.broadcasted_iota(jnp.int32, (TOK, 128), 1)
    hot = [jnp.where(lane == ids[:, k : k + 1], 1.0, 0.0) for k in range(2)]
    ordered = jnp.where(
        lax.broadcasted_iota(jnp.int32, (TOK, TOK), 1) < lax.broadcasted_iota(jnp.int32, (TOK, TOK), 0), 1.0, 0.0
    )
    before = dot(ordered.astype(BF), (hot[0] + hot[1]).astype(BF))
    col = lax.broadcasted_iota(jnp.int32, (TOK, ALL), 1).astype(F32)
    picks = []
    for k in range(2):
        e = ids[:, k : k + 1]
        plane = lax.shift_right_logical(e, 1)
        rel = plane - z
        rel = jnp.where(rel < 0, rel + PLANES, rel)
        base = rel * SLAB + (e - 2 * plane) * CAP
        place = jnp.sum(hot[k] * before, axis=1, keepdims=True)
        picks.append(jnp.where(col == base.astype(F32) + place, 1.0, 0.0).astype(BF))

    def from_slab(c):
        s = (c >= SLAB).astype(jnp.int32) + (c >= 2 * SLAB).astype(jnp.int32) + (c >= 3 * SLAB).astype(jnp.int32)
        rest = c - SLAB * s
        j = (rest >= CAP).astype(jnp.int32)
        row = j * ROWS + s * CAP + rest - CAP * j
        return jnp.where(rest < EXP * CAP, row, -1)

    into = jnp.where(
        from_slab(lax.broadcasted_iota(jnp.int32, (EXP * ROWS, ALL), 1))
        == lax.broadcasted_iota(jnp.int32, (EXP * ROWS, ALL), 0), 1.0, 0.0,
    ).astype(BF)
    back = jnp.where(
        from_slab(lax.broadcasted_iota(jnp.int32, (ALL, EXP * ROWS), 0))
        == lax.broadcasted_iota(jnp.int32, (ALL, EXP * ROWS), 1), 1.0, 0.0,
    ).astype(BF)

    net = Net(send, recv)
    pl.semaphore_wait(barrier, 8)
    go = net.go

    def slabs_out(rows, send_ref, arr_ref):
        for r in range(PLANES):
            part = rows[r * SLAB : (r + 1) * SLAB].astype(BF)
            if r == 0:
                arr_ref[0] = part
            else:
                send_ref[r] = part
        return [go(send_ref.at[r], arr_ref.at[PLANES - r], zs[r]) for r in (2, 1, 3)]

    slab_rows = dot((picks[0] + picks[1]), tok[...], (0, 0))
    zx = slabs_out(slab_rows, send_x, arr_x)

    def weight(k, lo):
        return wgu.at[:, :, pl.ds(lo + k * FP, FP)]

    def down(k):
        return wdn.at[:, pl.ds(k * FP, FP), :]

    cross = [go(wg, weight(1, 0), xc), go(wu, weight(1, HID), xc), go(wd, down(1), xc)]
    side = [go(wg, weight(2, 0), cp), go(wu, weight(2, HID), cp), go(wd, down(2), cp)]

    cotf = cot[...].astype(F32)
    rows_d = [(gw[:, k : k + 1] * cotf).astype(BF) for k in range(2)]
    zd = slabs_out(dot(picks[0], rows_d[0], (0, 0)) + dot(picks[1], rows_d[1], (0, 0)), send_d, arr_d)

    def chunk_in(arr_ref, g):
        rows = dot(into, arr_ref[...].reshape(ALL, D)).astype(BF)
        g[0, 0] = rows[:ROWS]
        g[1, 0] = rows[ROWS:]

    gx, gd = Gather(net, xg, xp, yu, yd), Gather(net, dg, xp, yu, yd)
    got(*zx)
    chunk_in(arr_x, xg)
    gx.start()
    got(*zd)
    chunk_in(arr_d, dg)
    gx.step2()
    gd.start()
    got(cross[0])
    side.append(go(weight(1, 0), weight(3, 0), cp))
    gx.step3()
    got(cross[1])
    side.append(go(weight(1, HID), weight(3, HID), cp))
    for copy in own:
        copy.wait()
    got(*side)

    def forward(e):
        def tile(n, _):
            cols = pl.ds(pl.multiple_of(n * 256, 256), 256)
            rows = xg[e].reshape(MINE, D)
            gate = dot(rows, wgu[e, :, cols])
            up = dot(rows, wgu[e, :, pl.ds(pl.multiple_of(n * 256 + HID, 256), 256)])
            sig = 1.0 / (1.0 + jnp.exp(-gate))
            act = gate * sig
            hid[e, :, cols] = (act * up).astype(BF)
            fac_b[e, :, cols] = act
            fac_a[e, :, cols] = up * sig * (1.0 + gate * (1.0 - sig))
            return 0

        lax.fori_loop(0, HID // 256, tile, 0)

    def project(e):
        def tile(n, _):
            cols = pl.ds(pl.multiple_of(n * 256, 256), 256)
            po[e, :, :, cols] = dot(hid[e], wdn[e, :, cols]).astype(BF).reshape(SLOTS, ROWS, 256)
            return 0

        lax.fori_loop(0, D // 256, tile, 0)

    gx.finish(0)
    forward(0)
    gd.step2()
    gx.finish(1)
    forward(1)
    gd.step3()
    got(cross[2])
    late = go(down(1), down(3), cp)
    got(late)
    ro = Reduce(net, po, near_o, far_o, across_o, xp, yu, yd)
    rv = Reduce(net, pv, near_v, far_v, across_v, xp, yu, yd)
    project(0)
    ro.start0()
    project(1)
    ro.start1()

    def backward(e):
        def tile(n, _):
            cols = pl.ds(pl.multiple_of(n * 256, 256), 256)
            dact = dot(dg[e].reshape(MINE, D), wdn[e, cols, :], (1, 1))
            dgu[e, :, cols] = (dact * fac_a[e, :, cols]).astype(BF)
            dgu[e, :, pl.ds(pl.multiple_of(n * 256 + HID, 256), 256)] = (dact * fac_b[e, :, cols]).astype(BF)
            return 0

        lax.fori_loop(0, HID // 256, tile, 0)

    def propagate(e):
        def tile(n, _):
            cols = pl.ds(pl.multiple_of(n * 256, 256), 256)
            part = dot(dgu[e], wgu[e, cols, :], (1, 1))
            pv[e, :, :, cols] = part.astype(BF).reshape(SLOTS, ROWS, 256)
            return 0

        lax.fori_loop(0, D // 256, tile, 0)

    def down_grad(e):
        def tile(n, _):
            cols = pl.ds(pl.multiple_of(n * 256, 256), 256)
            pd[e, cols, :] = dot(hid[e, :, cols], dg[e].reshape(MINE, D), (0, 0)).astype(BF)
            return 0

        lax.fori_loop(0, HID // 256, tile, 0)

    def up_grad(e):
        def tile(n, _):
            cols = pl.ds(pl.multiple_of(n * 256, 256), 256)
            pgu[e, cols, :] = dot(xg[e, :, :, cols].reshape(MINE, 256), dgu[e], (0, 0)).astype(BF)
            return 0

        lax.fori_loop(0, D // 256, tile, 0)

    gd.finish(0)
    backward(0)
    gd.finish(1)
    backward(1)
    ro.step2()
    propagate(0)
    rv.start0()
    propagate(1)
    rv.start1()
    ro.step3()
    for e in range(EXP):
        down_grad(e)

    pair = 2 * FP
    share_d = go(pd.at[:, pl.ds(pair, pair), :], rd, cp)
    rv.step2()
    for e in range(EXP):
        up_grad(e)
    share_g = go(pgu.at[:, :, pl.ds(pair, pair)], rgu.at[0], cp)
    share_u = go(pgu.at[:, :, pl.ds(HID + pair, pair)], rgu.at[1], cp)
    got(share_d)
    pd[:, pl.ds(0, pair), :] = (pd[:, pl.ds(0, pair), :].astype(F32) + rd[...].astype(F32)).astype(BF)
    far_d = go(pd.at[:, pl.ds(FP, FP), :], rd2, xc)
    far_g = []
    for i, share in ((0, share_g), (1, share_u)):
        got(share)
        cols = pl.ds(i * HID, pair)

        def add(e, _, i=i, cols=cols):
            pgu[e, :, cols] = (pgu[e, :, cols].astype(F32) + rgu[i, e].astype(F32)).astype(BF)
            return 0

        lax.fori_loop(0, EXP, add, 0)
        far_g.append(go(pgu.at[:, :, pl.ds(i * HID + FP, FP)], rgu2.at[i], xc))
    rv.step3()

    def results_back(rows, send_ref, arr_ref):
        return slabs_out(dot(back, rows), send_ref, arr_ref)

    zo = results_back(ro.step4(), send_o, arr_o)
    zv = results_back(rv.step4(), send_v, arr_v)
    got(*zo)
    rows = arr_o[...].reshape(ALL, D)
    mixed[...] = (gw[:, 0:1] * dot(picks[0], rows) + gw[:, 1:2] * dot(picks[1], rows)).astype(BF)
    got(*zv)
    gtok[...] = dot(picks[0] + picks[1], arr_v[...].reshape(ALL, D)).astype(BF)
    got(far_d)
    gdown[...] = (pd[:, pl.ds(0, FP), :].astype(F32) + rd2[...].astype(F32)).astype(BF)
    for i, out in ((0, ggate), (1, gup)):
        got(far_g[i])
        out[...] = (pgu[:, :, pl.ds(i * HID, FP)].astype(F32) + rgu2[i].astype(F32)).astype(BF)
    for copy in net.all:
        copy.wait_send()


def body(tokens, expert_ids, gate_weights, w_gate, w_up, w_down, cotangent):
    vmem, hbm = pl.BlockSpec(memory_space=pltpu.VMEM), pl.BlockSpec(memory_space=pl.ANY)

    def buf(*shape, dtype=BF):
        return pltpu.VMEM(shape, dtype)

    slab = [buf(PLANES, SLAB, D) for _ in range(8)]
    big = [buf(EXP, SLOTS, ROWS, D) for _ in range(4)]
    rings = [buf(3, 2, ROWS, HALF), buf(3, 2, ROWS, D), buf(5, ROWS, D)] * 2
    scratch = slab + big + rings + [
        buf(EXP, D, 2 * HID), buf(EXP, HID, D),
        buf(EXP, MINE, HID, dtype=F32), buf(EXP, MINE, HID, dtype=F32),
        buf(EXP, MINE, HID), buf(EXP, MINE, 2 * HID),
        buf(EXP, HID, D), buf(EXP, D, 2 * HID),
        buf(EXP, 2 * FP, D), buf(2, EXP, D, 2 * FP), buf(EXP, FP, D), buf(2, EXP, D, FP),
        pltpu.SemaphoreType.DMA((COPIES,)), pltpu.SemaphoreType.DMA((COPIES,)), pltpu.SemaphoreType.DMA((3,)),
    ]
    return pl.pallas_call(
        kernel,
        out_shape=tuple(
            jax.ShapeDtypeStruct(a.shape, BF) for a in (tokens, tokens, w_gate, w_up, w_down)
        ),
        in_specs=[vmem] * 4 + [hbm] * 3,
        out_specs=(vmem,) * 5,
        scratch_shapes=scratch,
        compiler_params=pltpu.CompilerParams(
            collective_id=0, has_side_effects=True, vmem_limit_bytes=67043328
        ),
    )(tokens, expert_ids, gate_weights, cotangent, w_gate, w_up, w_down)


def solution(mesh):
    rows = P(("dp", "expert"), None)
    cols = P("expert", None, "dp")
    down = P("expert", "dp", None)
    return jax.shard_map(
        body,
        mesh=mesh,
        in_specs=(rows, rows, rows, cols, cols, down, rows),
        out_specs=(rows, rows, cols, cols, down),
        check_vma=False,
    )
```

time: 349 us -> 146 us (0.42); the launches traced: 345 us -> 146 us
  waiting for transfers between devices: 236 us -> 0 us
  Pallas kernels: 0 us -> 137 us
  matrix products: 41.8 us -> 0 us
  blocking collectives: 20.1 us -> 0 us
  between operations: 14.2 us -> 0.66 us
  starting transfers between devices: 13.3 us -> 0 us
  local copies, waits for them, and re-layouts: 14.4 us -> 8.55 us
  other arithmetic: 5.69 us -> 0 us
    unnamed x4 -> x0, waiting for transfers between devices: 139 us -> none
    pallas_call x0 -> x1, Pallas kernels: none -> 137 us  [body(): pl.pallas_call(kernel, out_shape=tuple((jax.ShapeDtypeStruct(a.shape, BF)...]
    all_gather x2 -> x0, waiting for transfers between devices: 89.8 us -> none  [spread(): lax.all_gather(arrived, 'dp', axis=0, tiled=False, axis_index_groups=same...]
    dot_general x13 -> x0, matrix products: 41.8 us -> none  [the longest x1 7.12 us: body(): jnp.einsum('pjcd,jfd->pjcf', ds, wd, preferred_element_type=jnp.float32)]
    all_to_all x2 -> x0, blocking collectives: 20.1 us -> none  [spread(): lax.all_to_all(buffer, 'expert', split_axis=0, concat_axis=0, tiled=True)]
    all_to_all x2 -> x0, starting transfers between devices: 7.59 us -> none  [collect(): lax.all_to_all(summed, 'expert', split_axis=0, concat_axis=0, tiled=True)]
    all_to_all x2 -> x0, waiting for transfers between devices: 6.25 us -> none  [collect(): lax.all_to_all(summed, 'expert', split_axis=0, concat_axis=0, tiled=True)]
    ppermute x6 -> x0, starting transfers between devices: 5.57 us -> none  [other(): return lax.ppermute(v, 'dp', swap)]
  transfers between devices with their start and end apart: 11 -> 0, of which waited for: 6 -> 0; matrix products, arithmetic and copies ran while one was open for 10% -> 0% of each run, Pallas kernels for 0% -> 0%
where the time goes in v2:
time: 146 us
  Pallas kernels  137 us (94%)
  local copies, waits for them, and re-layouts  8.55 us (6%)
    pallas_call x1, Pallas kernels, body(): pl.pallas_call(kernel, out_shape=tuple((jax.ShapeDtypeStruct(a.shape, BF)...  137 us
    unnamed x15, local copies, waits for them, and re-layouts  8.55 us

profile of v2, /device:TPU:1, one launch (start us, length us, event | category | flops | bytes accessed | tf_op | source)
XLA Modules:
  0.0 145.8 jit_solution(6545512782071591433)
XLA Ops:
  0.6 0.0 copy-start.3
  0.6 1.4 copy.12.ids
  2.0 0.0 copy-done.3
  2.0 0.7 copy.13.gw
  2.7 136.6 %shard_map.110 = (bf16[64,1024]{1,0:T(8,128)(2,1)}, bf16[64,1024]{1,0:T(8,128)(2,1)}, bf16[2,1024,128]{2,1,0:T(8,128)(2,1)}, bf16[2,1024,128]{2,1,0:T(8,128)(2,1)}, bf16[2,128,1024]{2,1,0:T(8,128)(2,1)}) custom-call(bf16[64,1024]{1,0:T(8,128)(2,1)} %tok.1, s32[64,2]{1,0:T(8,128)} %copy.12.ids, f32[64,2]{1,0:T(8,128)} %copy.13.gw, bf16[64,1024]{1,0:T(8,128)(2,1)} %cot.1, ...), custom_call_target="tpu_custom_call" | custom-call | tf_op jit(solution)/shard_map/pallas_call | solution.py:438
  139.4 0.0 copy-start.2
  139.4 1.6 %copy.19 = bf16[64,1024]{1,0:T(8,128)(2,1)} copy(bf16[64,1024]{1,0:T(8,128)(2,1)} %get-tuple-element.10) | data formatting | bytes 262144
  141.0 1.6 %copy.20 = bf16[64,1024]{1,0:T(8,128)(2,1)} copy(bf16[64,1024]{1,0:T(8,128)(2,1)} %get-tuple-element.11) | data formatting | bytes 262144
  142.6 0.0 copy-done.2
  142.6 0.0 copy-start.1
  142.6 0.8 copy.21
  143.4 0.4 copy-done.1
  143.8 0.0 copy-start
  143.8 0.8 copy.22
  144.6 0.4 copy-done
  145.0 0.8 copy.23
Async XLA Ops:
  0.6 1.4 copy-start.3
  139.4 3.2 %copy-start.2 = (bf16[2,1024,128]{2,1,0:T(8,128)(2,1)S(1)}, bf16[2,1024,128]{2,1,0:T(8,128)(2,1)}, u32[]{:S(2)}) copy-start(bf16[2,1024,128]{2,1,0:T(8,128)(2,1)} %get-tuple-element.12) | copy-start | bytes 1572868
  142.6 1.2 copy-start.1
  143.8 1.2 copy-start

commit v3 on v2

--- a/solution.py
+++ b/solution.py
@@ -175,10 +175,10 @@
 
 def kernel(
     tok, ids, gw, cot, wg, wu, wd,
-    mixed, gtok, ggate, gup, gdown,
-    send_x, send_d, arr_x, arr_d, send_o, send_v, arr_o, arr_v,
+    pick, arr_o, arr_v, sum_d, sum_gu, far_d, far_gu,
+    send_x, send_d, send_o, send_v, arr_x, arr_d, via,
     xg, dg, po, pv, near_o, far_o, across_o, near_v, far_v, across_v,
-    wgu, wdn, fac_a, fac_b, hid, dgu, pd, pgu, rd, rgu, rd2, rgu2,
+    wgu, wdn, fac_a, fac_b, hid, dgu, pd, pgu, rd, rgu,
     send, recv, local,
 ):
     dp, z = lax.axis_index("dp"), lax.axis_index("expert")
@@ -205,22 +205,22 @@
     for copy in own:
         copy.start()
 
-    lane = lax.broadcasted_iota(jnp.int32, (TOK, 128), 1)
-    hot = [jnp.where(lane == ids[:, k : k + 1], 1.0, 0.0) for k in range(2)]
-    ordered = jnp.where(
-        lax.broadcasted_iota(jnp.int32, (TOK, TOK), 1) < lax.broadcasted_iota(jnp.int32, (TOK, TOK), 0), 1.0, 0.0
-    )
-    before = dot(ordered.astype(BF), (hot[0] + hot[1]).astype(BF))
-    col = lax.broadcasted_iota(jnp.int32, (TOK, ALL), 1).astype(F32)
+    expert = lax.broadcasted_iota(jnp.int32, (2 * PLANES, TOK), 0)
+    hot = [jnp.where(expert == ids[k : k + 1, :], 1.0, 0.0) for k in range(2)]
+    row_t = lax.broadcasted_iota(jnp.int32, (TOK, TOK), 0)
+    col_t = lax.broadcasted_iota(jnp.int32, (TOK, TOK), 1)
+    before = dot((hot[0] + hot[1]).astype(BF), jnp.where(row_t < col_t, 1.0, 0.0).astype(BF))
+    slab_row = lax.broadcasted_iota(jnp.int32, (ALL, TOK), 0).astype(F32)
     picks = []
     for k in range(2):
-        e = ids[:, k : k + 1]
+        e = ids[k : k + 1, :]
         plane = lax.shift_right_logical(e, 1)
         rel = plane - z
         rel = jnp.where(rel < 0, rel + PLANES, rel)
         base = rel * SLAB + (e - 2 * plane) * CAP
-        place = jnp.sum(hot[k] * before, axis=1, keepdims=True)
-        picks.append(jnp.where(col == base.astype(F32) + place, 1.0, 0.0).astype(BF))
+        place = jnp.sum(hot[k] * before, axis=0, keepdims=True)
+        picks.append(jnp.where(slab_row == base.astype(F32) + place, 1.0, 0.0).astype(BF))
+        pick[k] = picks[k]
 
     def from_slab(c):
         s = (c >= SLAB).astype(jnp.int32) + (c >= 2 * SLAB).astype(jnp.int32) + (c >= 3 * SLAB).astype(jnp.int32)
@@ -242,17 +242,34 @@
     pl.semaphore_wait(barrier, 8)
     go = net.go
 
-    def slabs_out(rows, send_ref, arr_ref):
-        for r in range(PLANES):
-            part = rows[r * SLAB : (r + 1) * SLAB].astype(BF)
-            if r == 0:
-                arr_ref[0] = part
-            else:
-                send_ref[r] = part
-        return [go(send_ref.at[r], arr_ref.at[PLANES - r], zs[r]) for r in (2, 1, 3)]
-
-    slab_rows = dot((picks[0] + picks[1]), tok[...], (0, 0))
-    zx = slabs_out(slab_rows, send_x, arr_x)
+    class Exchange:
+        def __init__(self, rows, send_ref, arr_ref, via_ref, keep=None):
+            for r in range(PLANES):
+                part = rows[r * SLAB : (r + 1) * SLAB].astype(BF)
+                if r == 0 and keep is None:
+                    arr_ref[0] = part
+                else:
+                    send_ref[r] = part
+            self.send, self.arr, self.via, self.keep = send_ref, arr_ref, via_ref, keep
+
+        def start(self):
+            lo, hi = pl.ds(0, HALF), pl.ds(HALF, HALF)
+            self.first = go(self.send.at[2, :, hi], self.via, zs[3])
+            self.copies = [go(self.send.at[2, :, lo], self.arr.at[2, :, lo], zs[2])]
+            self.copies += [go(self.send.at[r], self.arr.at[PLANES - r], zs[r]) for r in (3, 1)]
+            if self.keep is not None:
+                self.own = pltpu.make_async_copy(self.send.at[0], self.arr.at[0], self.keep)
+                self.own.start()
+
+        def forward(self):
+            got(self.first)
+            self.copies.append(go(self.via, self.arr.at[2, :, pl.ds(HALF, HALF)], zs[3]))
+
+        def finish(self):
+            got(*self.copies)
+
+    ex = Exchange(dot(picks[0] + picks[1], tok[...]), send_x, arr_x, via.at[0])
+    ex.start()
 
     def weight(k, lo):
         return wgu.at[:, :, pl.ds(lo + k * FP, FP)]
@@ -264,8 +281,9 @@
     side = [go(wg, weight(2, 0), cp), go(wu, weight(2, HID), cp), go(wd, down(2), cp)]
 
     cotf = cot[...].astype(F32)
-    rows_d = [(gw[:, k : k + 1] * cotf).astype(BF) for k in range(2)]
-    zd = slabs_out(dot(picks[0], rows_d[0], (0, 0)) + dot(picks[1], rows_d[1], (0, 0)), send_d, arr_d)
+    rows_d = [(jnp.sum(jnp.where(row_t == col_t, gw[k : k + 1, :], 0.0), axis=1, keepdims=True) * cotf).astype(BF) for k in range(2)]
+    ed = Exchange(dot(picks[0], rows_d[0]) + dot(picks[1], rows_d[1]), send_d, arr_d, via.at[1])
+    ex.forward()
 
     def chunk_in(arr_ref, g):
         rows = dot(into, arr_ref[...].reshape(ALL, D)).astype(BF)
@@ -273,12 +291,14 @@
         g[1, 0] = rows[ROWS:]
 
     gx, gd = Gather(net, xg, xp, yu, yd), Gather(net, dg, xp, yu, yd)
-    got(*zx)
+    ex.finish()
     chunk_in(arr_x, xg)
     gx.start()
-    got(*zd)
+    ed.start()
+    gx.step2()
+    ed.forward()
+    ed.finish()
     chunk_in(arr_d, dg)
-    gx.step2()
     gd.start()
     got(cross[0])
     side.append(go(weight(1, 0), weight(3, 0), cp))
@@ -363,90 +383,133 @@
 
         lax.fori_loop(0, D // 256, tile, 0)
 
+    pair = 2 * FP
+    share, kept = {}, []
+
+    def keep(src, dst):
+        copy = pltpu.make_async_copy(src, dst, local.at[3 + len(kept)])
+        copy.start()
+        kept.append(copy)
+
+    def share_down(e):
+        share["d", e] = go(pd.at[e, pl.ds(pair, pair), :], rd.at[e], cp)
+
+    def share_up(e):
+        for i in range(2):
+            share[i, e] = go(pgu.at[e, :, pl.ds(i * HID + pair, pair)], rgu.at[i, e], cp)
+
+    far = []
+
+    def send_down(e):
+        got(share["d", e])
+        pd[e, pl.ds(0, pair), :] = (pd[e, pl.ds(0, pair), :].astype(F32) + rd[e].astype(F32)).astype(BF)
+        far.append(go(pd.at[e, pl.ds(FP, FP), :], far_d.at[e], xc))
+        keep(pd.at[e, pl.ds(0, FP), :], sum_d.at[e])
+
+    def send_up(e):
+        for i in range(2):
+            got(share[i, e])
+            cols = pl.ds(i * HID, pair)
+            pgu[e, :, cols] = (pgu[e, :, cols].astype(F32) + rgu[i, e].astype(F32)).astype(BF)
+            far.append(go(pgu.at[e, :, pl.ds(i * HID + FP, FP)], far_gu.at[i, e], xc))
+            keep(pgu.at[e, :, pl.ds(i * HID, FP)], sum_gu.at[i, e])
+
     gd.finish(0)
     backward(0)
+    down_grad(0)
+    share_down(0)
     gd.finish(1)
     backward(1)
     ro.step2()
+    down_grad(1)
+    share_down(1)
+    send_down(0)
+    up_grad(0)
+    share_up(0)
+    send_down(1)
+    ro.step3()
+    up_grad(1)
+    share_up(1)
+    send_up(0)
     propagate(0)
     rv.start0()
+    send_up(1)
     propagate(1)
     rv.start1()
-    ro.step3()
-    for e in range(EXP):
-        down_grad(e)
-
-    pair = 2 * FP
-    share_d = go(pd.at[:, pl.ds(pair, pair), :], rd, cp)
+    eo = Exchange(dot(back, ro.step4()), send_o, arr_o, via.at[2], local.at[9])
+    eo.start()
     rv.step2()
-    for e in range(EXP):
-        up_grad(e)
-    share_g = go(pgu.at[:, :, pl.ds(pair, pair)], rgu.at[0], cp)
-    share_u = go(pgu.at[:, :, pl.ds(HID + pair, pair)], rgu.at[1], cp)
-    got(share_d)
-    pd[:, pl.ds(0, pair), :] = (pd[:, pl.ds(0, pair), :].astype(F32) + rd[...].astype(F32)).astype(BF)
-    far_d = go(pd.at[:, pl.ds(FP, FP), :], rd2, xc)
-    far_g = []
-    for i, share in ((0, share_g), (1, share_u)):
-        got(share)
-        cols = pl.ds(i * HID, pair)
-
-        def add(e, _, i=i, cols=cols):
-            pgu[e, :, cols] = (pgu[e, :, cols].astype(F32) + rgu[i, e].astype(F32)).astype(BF)
-            return 0
-
-        lax.fori_loop(0, EXP, add, 0)
-        far_g.append(go(pgu.at[:, :, pl.ds(i * HID + FP, FP)], rgu2.at[i], xc))
+    eo.forward()
     rv.step3()
-
-    def results_back(rows, send_ref, arr_ref):
-        return slabs_out(dot(back, rows), send_ref, arr_ref)
-
-    zo = results_back(ro.step4(), send_o, arr_o)
-    zv = results_back(rv.step4(), send_v, arr_v)
-    got(*zo)
-    rows = arr_o[...].reshape(ALL, D)
-    mixed[...] = (gw[:, 0:1] * dot(picks[0], rows) + gw[:, 1:2] * dot(picks[1], rows)).astype(BF)
-    got(*zv)
-    gtok[...] = dot(picks[0] + picks[1], arr_v[...].reshape(ALL, D)).astype(BF)
-    got(far_d)
-    gdown[...] = (pd[:, pl.ds(0, FP), :].astype(F32) + rd2[...].astype(F32)).astype(BF)
-    for i, out in ((0, ggate), (1, gup)):
-        got(far_g[i])
-        out[...] = (pgu[:, :, pl.ds(i * HID, FP)].astype(F32) + rgu2[i].astype(F32)).astype(BF)
+    ev = Exchange(dot(back, rv.step4()), send_v, arr_v, via.at[3], local.at[10])
+    ev.start()
+    eo.finish()
+    ev.forward()
+    ev.finish()
+    got(*far)
+    for copy in kept + [eo.own, ev.own]:
+        copy.wait()
     for copy in net.all:
         copy.wait_send()
 
 
+def finish(gw, pick, arr_o, arr_v, sum_d, sum_gu, far_d, far_gu, mixed, gtok, ggate, gup, gdown):
+    eye = lax.broadcasted_iota(jnp.int32, (TOK, TOK), 0) == lax.broadcasted_iota(jnp.int32, (TOK, TOK), 1)
+    rows = arr_o[...].reshape(ALL, D)
+    total = jnp.zeros((TOK, D), F32)
+    for k in range(2):
+        weight = jnp.sum(jnp.where(eye, gw[k : k + 1, :], 0.0), axis=1, keepdims=True)
+        total = total + weight * dot(pick[k], rows, (0, 0))
+    mixed[...] = total.astype(BF)
+    gtok[...] = dot(pick[0] + pick[1], arr_v[...].reshape(ALL, D), (0, 0)).astype(BF)
+    gdown[...] = (sum_d[...].astype(F32) + far_d[...].astype(F32)).astype(BF)
+    ggate[...] = (sum_gu[0].astype(F32) + far_gu[0].astype(F32)).astype(BF)
+    gup[...] = (sum_gu[1].astype(F32) + far_gu[1].astype(F32)).astype(BF)
+
+
 def body(tokens, expert_ids, gate_weights, w_gate, w_up, w_down, cotangent):
     vmem, hbm = pl.BlockSpec(memory_space=pltpu.VMEM), pl.BlockSpec(memory_space=pl.ANY)
 
     def buf(*shape, dtype=BF):
         return pltpu.VMEM(shape, dtype)
 
-    slab = [buf(PLANES, SLAB, D) for _ in range(8)]
+    slab = [buf(PLANES, SLAB, D) for _ in range(6)]
     big = [buf(EXP, SLOTS, ROWS, D) for _ in range(4)]
     rings = [buf(3, 2, ROWS, HALF), buf(3, 2, ROWS, D), buf(5, ROWS, D)] * 2
-    scratch = slab + big + rings + [
+    scratch = slab + [buf(4, SLAB, HALF)] + big + rings + [
         buf(EXP, D, 2 * HID), buf(EXP, HID, D),
         buf(EXP, MINE, HID, dtype=F32), buf(EXP, MINE, HID, dtype=F32),
         buf(EXP, MINE, HID), buf(EXP, MINE, 2 * HID),
         buf(EXP, HID, D), buf(EXP, D, 2 * HID),
-        buf(EXP, 2 * FP, D), buf(2, EXP, D, 2 * FP), buf(EXP, FP, D), buf(2, EXP, D, FP),
-        pltpu.SemaphoreType.DMA((COPIES,)), pltpu.SemaphoreType.DMA((COPIES,)), pltpu.SemaphoreType.DMA((3,)),
+        buf(EXP, 2 * FP, D), buf(2, EXP, D, 2 * FP),
+        pltpu.SemaphoreType.DMA((COPIES,)), pltpu.SemaphoreType.DMA((COPIES,)), pltpu.SemaphoreType.DMA((11,)),
     ]
-    return pl.pallas_call(
+
+    def out(*shape):
+        return jax.ShapeDtypeStruct(shape, BF)
+
+    weights = gate_weights.T
+    parts = pl.pallas_call(
         kernel,
-        out_shape=tuple(
-            jax.ShapeDtypeStruct(a.shape, BF) for a in (tokens, tokens, w_gate, w_up, w_down)
+        out_shape=(
+            out(2, ALL, TOK), out(PLANES, SLAB, D), out(PLANES, SLAB, D),
+            out(EXP, FP, D), out(2, EXP, D, FP), out(EXP, FP, D), out(2, EXP, D, FP),
         ),
         in_specs=[vmem] * 4 + [hbm] * 3,
-        out_specs=(vmem,) * 5,
+        out_specs=(vmem,) + (hbm,) * 6,
         scratch_shapes=scratch,
         compiler_params=pltpu.CompilerParams(
             collective_id=0, has_side_effects=True, vmem_limit_bytes=67043328
         ),
-    )(tokens, expert_ids, gate_weights, cotangent, w_gate, w_up, w_down)
+    )(tokens, expert_ids.T, weights, cotangent, w_gate, w_up, w_down)
+    return pl.pallas_call(
+        finish,
+        out_shape=tuple(
+            jax.ShapeDtypeStruct(a.shape, BF) for a in (tokens, tokens, w_gate, w_up, w_down)
+        ),
+        in_specs=[vmem] * 8,
+        out_specs=(vmem,) * 5,
+    )(weights, *parts)
 
 
 def solution(mesh):

time: 146 us -> 116 us (0.79)
  Pallas kernels: 137 us -> 115 us
  local copies, waits for them, and re-layouts: 8.55 us -> 0 us
    pallas_call x1 -> x2, Pallas kernels: 137 us -> 115 us  [the longest x1 110 us: body(): pl.pallas_call(kernel, out_shape=(out(2, ALL, TOK), out(PLANES, SLAB, D),...]
    unnamed x15 -> x0, local copies, waits for them, and re-layouts: 8.55 us -> none
where the time goes in v3:
time: 116 us; the launch traced here: 115 us
  Pallas kernels  115 us (99%)
    pallas_call x1, Pallas kernels, body(): pl.pallas_call(kernel, out_shape=(out(2, ALL, TOK), out(PLANES, SLAB, D),...  110 us
    pallas_call x1, Pallas kernels, body(): pl.pallas_call(finish, out_shape=tuple((jax.ShapeDtypeStruct(a.shape, BF)...  4.04 us

profile of v3, /device:TPU:1, one launch (start us, length us, event | category | flops | bytes accessed | tf_op | source)
XLA Modules:
  0.0 115.2 jit_solution(6344496702137154925)
XLA Ops:
  0.6 110.5 %shard_map.110 = (bf16[2,192,64]{2,1,0:T(8,128)(2,1)}, bf16[4,48,1024]{2,1,0:T(8,128)(2,1)}, bf16[4,48,1024]{2,1,0:T(8,128)(2,1)}, bf16[2,128,1024]{2,1,0:T(8,12...) custom-call(bf16[64,1024]{1,0:T(8,128)(2,1)} %tok.1, ...), custom_call_target="tpu_custom_call" | custom-call | tf_op jit(solution)/shard_map/pallas_call | solution.py:492
  111.1 4.0 %shard_map.111 = (bf16[64,1024]{1,0:T(8,128)(2,1)}, bf16[64,1024]{1,0:T(8,128)(2,1)}, bf16[2,1024,128]{2,1,0:T(8,128)(2,1)}, bf16[2,1024,128]{2,1,0:T(8,128)(2,1)}, bf16[2,128,1024]{2,1,0:T(8,128)(2,1)}) custom-call(f32[2,64]{1,0:T(2,128)} %bitcast.3, bf16[2,192,64]{2,1,0:T(8,128)(2,1)} %get-tuple-element.12.pick, ...), custom_call_target="tpu_custom_call" | custom-call | tf_op jit(solution)/shard_map/pallas_call | solution.py:505

commit v4 on v3

--- a/solution.py
+++ b/solution.py
@@ -17,7 +17,7 @@
 HALF = D // 2
 FP = 128
 HID = 4 * FP
-COPIES = 128
+COPIES = 144
 
 
 def dot(a, b, contract=(1, 0)):
@@ -44,62 +44,66 @@
         copy.wait_recv()
 
 
-def left(ref, e, s):
-    return ref.at[e, s, :, pl.ds(0, HALF)]
-
-
-def right(ref, e, s):
-    return ref.at[e, s, :, pl.ds(HALF, HALF)]
+def wide(u):
+    return pl.ds(u * HALF, HALF)
+
+
+def full(ref, u, s):
+    return ref.at[:, s, :, wide(u)]
+
+
+def half(ref, u, s, e):
+    return ref.at[e, s, :, wide(u)]
 
 
 class Gather:
     def __init__(self, net, ref, xp, yu, yd):
         self.net, self.ref, self.xp, self.yu, self.yd = net, ref, xp, yu, yd
 
-    def start(self):
-        go, g = self.net.go, self.ref
-        self.x0 = go(g.at[0, 0], g.at[0, 4], self.xp)
-        self.u1 = go(g.at[1, 0], g.at[1, 3], self.yu)
-        self.d1 = go(g.at[1, 0], g.at[1, 1], self.yd)
-        self.u00 = go(g.at[0, 0], g.at[0, 3], self.yu)
-        self.d00 = go(g.at[0, 0], g.at[0, 1], self.yd)
-        self.x1 = [go(g.at[1, 0], g.at[1, 4], self.xp)]
-
-    def step2(self):
-        go, g = self.net.go, self.ref
+    def move(self, u, src, dst, to):
+        return self.net.go(full(self.ref, u, src), full(self.ref, u, dst), to)
+
+    def pass_on(self, u, src, dst, e, to):
+        return self.net.go(half(self.ref, u, src, e), half(self.ref, u, dst, e), to)
+
+    def start0(self):
+        self.x0 = self.move(0, 0, 4, self.xp)
+        self.u00 = self.move(0, 0, 3, self.yu)
+        self.d00 = self.move(0, 0, 1, self.yd)
+
+    def start1(self):
+        self.u1 = self.move(1, 0, 3, self.yu)
+        self.d1 = self.move(1, 0, 1, self.yd)
+        self.x1 = [self.move(1, 0, 4, self.xp)]
+
+    def step2a(self):
         got(self.x0)
-        self.u01 = go(g.at[0, 4], g.at[0, 7], self.yu)
-        self.d01 = go(g.at[0, 4], g.at[0, 5], self.yd)
+        self.u01 = self.move(0, 4, 7, self.yu)
+        self.d01 = self.move(0, 4, 5, self.yd)
+
+    def step2b(self):
         got(self.u1)
-        self.fu1 = go(left(g, 1, 3), left(g, 1, 2), self.yu)
-        self.x1.append(go(g.at[1, 3], g.at[1, 7], self.xp))
+        self.fu1 = self.pass_on(1, 3, 2, 0, self.yu)
+        self.x1.append(self.move(1, 3, 7, self.xp))
         got(self.d1)
-        self.fd1 = go(right(g, 1, 1), right(g, 1, 2), self.yd)
-        self.x1.append(go(g.at[1, 1], g.at[1, 5], self.xp))
+        self.fd1 = self.pass_on(1, 1, 2, 1, self.yd)
+        self.x1.append(self.move(1, 1, 5, self.xp))
         got(self.u00)
-        self.fu00 = go(left(g, 0, 3), left(g, 0, 2), self.yu)
+        self.fu00 = self.pass_on(0, 3, 2, 0, self.yu)
         got(self.d00)
-        self.fd00 = go(right(g, 0, 1), right(g, 0, 2), self.yd)
+        self.fd00 = self.pass_on(0, 1, 2, 1, self.yd)
 
     def step3(self):
-        go, g = self.net.go, self.ref
+        got(self.fu1, self.fd1)
+        self.x1.append(self.move(1, 2, 6, self.xp))
         got(self.u01)
-        self.fu01 = go(left(g, 0, 7), left(g, 0, 6), self.yu)
+        self.fu01 = self.pass_on(0, 7, 6, 0, self.yu)
         got(self.d01)
-        self.fd01 = go(right(g, 0, 5), right(g, 0, 6), self.yd)
-        got(self.fu1, self.fd1)
-        self.x1.append(go(g.at[1, 2], g.at[1, 6], self.xp))
-
-    def finish(self, e):
-        if e == 0:
-            got(self.fu00, self.fd00, self.fu01, self.fd01)
-        else:
-            got(*self.x1)
-
-
-def add_half(p, e, s, lo, arrived):
-    cols = pl.ds(lo, HALF)
-    p[e, s, :, cols] = (p[e, s, :, cols].astype(F32) + arrived[...].astype(F32)).astype(BF)
+        self.fd01 = self.pass_on(0, 5, 6, 1, self.yd)
+
+    def finish(self):
+        got(self.fu00, self.fd00, self.fu01, self.fd01)
+        got(*self.x1)
 
 
 class Reduce:
@@ -108,32 +112,34 @@
         self.xp, self.yu, self.yd = xp, yu, yd
         self.ring = {}
 
-    def outer(self, key, e, b):
-        go, p = self.net.go, self.p
+    def outer(self, key, u, b):
         self.ring[key] = [
-            go(left(p, e, b + 2), self.near.at[key, 0], self.yu),
-            go(right(p, e, b + 2), self.near.at[key, 1], self.yd),
+            self.net.go(half(self.p, u, b + 2, 0), self.near.at[key, 0], self.yu),
+            self.net.go(half(self.p, u, b + 2, 1), self.near.at[key, 1], self.yd),
         ]
 
-    def free_up(self, key, e, b):
-        self.ring[key].append(self.net.go(right(self.p, e, b + 1), right(self.far, key, 0), self.yu))
-
-    def free_down(self, key, e, b):
-        self.ring[key].append(self.net.go(left(self.p, e, b + 3), left(self.far, key, 1), self.yd))
-
-    def inner(self, key, e, b):
-        go, p = self.net.go, self.p
+    def free_up(self, key, u, b):
+        self.ring[key].append(self.net.go(half(self.p, u, b + 1, 1), self.far.at[key, 0, 1], self.yu))
+
+    def free_down(self, key, u, b):
+        self.ring[key].append(self.net.go(half(self.p, u, b + 3, 0), self.far.at[key, 1, 0], self.yd))
+
+    def add(self, e, s, u, arrived):
+        cols = wide(u)
+        self.p[e, s, :, cols] = (self.p[e, s, :, cols].astype(F32) + arrived.astype(F32)).astype(BF)
+
+    def inner(self, key, u, b):
         got(self.ring[key][0])
-        add_half(p, e, b + 1, 0, self.near.at[key, 0])
-        up = go(left(p, e, b + 1), left(self.far, key, 0), self.yu)
+        self.add(0, b + 1, u, self.near[key, 0])
+        up = self.net.go(half(self.p, u, b + 1, 0), self.far.at[key, 0, 0], self.yu)
         got(self.ring[key][1])
-        add_half(p, e, b + 3, HALF, self.near.at[key, 1])
-        down = go(right(p, e, b + 3), right(self.far, key, 1), self.yd)
+        self.add(1, b + 3, u, self.near[key, 1])
+        down = self.net.go(half(self.p, u, b + 3, 1), self.far.at[key, 1, 1], self.yd)
         self.ring[key] += [up, down]
 
-    def total(self, key, e, b):
+    def total(self, key, u, b):
         got(*self.ring[key][2:])
-        return self.p[e, b].astype(F32) + self.far[key, 0].astype(F32) + self.far[key, 1].astype(F32)
+        return self.p[:, b, :, wide(u)].astype(F32) + self.far[key, 0].astype(F32) + self.far[key, 1].astype(F32)
 
     def start0(self):
         for dx in (1, 0):
@@ -143,34 +149,38 @@
             self.free_down(dx, 0, 4 * dx)
 
     def start1(self):
-        self.x1 = {dy: self.net.go(self.p.at[1, 4 + dy], self.across.at[dy], self.xp) for dy in (2, 1, 3, 0)}
+        self.x1 = {dy: self.net.go(full(self.p, 1, 4 + dy), self.across.at[dy], self.xp) for dy in (2, 1, 3, 0)}
 
     def joined(self, dy):
         got(self.x1[dy])
-        self.p[1, dy] = (self.p[1, dy].astype(F32) + self.across[dy].astype(F32)).astype(BF)
-
-    def step2(self):
+        for e in range(EXP):
+            self.add(e, dy, 1, self.across[dy, e])
+
+    def step_a(self):
         self.joined(2)
         self.outer(2, 1, 0)
         self.inner(1, 0, 4)
+
+    def step_b(self):
         self.inner(0, 0, 0)
         self.joined(1)
         self.free_up(2, 1, 0)
+
+    def step_c(self):
+        self.p[:, 4, :, wide(0)] = self.total(1, 0, 4).astype(BF)
+        self.x0 = self.net.go(full(self.p, 0, 4), self.across.at[4], self.xp)
         self.joined(3)
         self.free_down(2, 1, 0)
+        self.inner(2, 1, 0)
+
+    def final0(self):
+        rows = self.total(0, 0, 0)
+        got(self.x0)
+        return (rows + self.across[4].astype(F32)).astype(BF).reshape(EXP * ROWS, HALF)
+
+    def final1(self):
         self.joined(0)
-
-    def step3(self):
-        self.p[0, 4] = self.total(1, 0, 4).astype(BF)
-        self.x0 = self.net.go(self.p.at[0, 4], self.across.at[4], self.xp)
-        self.inner(2, 1, 0)
-
-    def step4(self):
-        rows0 = self.total(0, 0, 0)
-        got(self.x0)
-        rows0 = (rows0 + self.across[4].astype(F32)).astype(BF)
-        rows1 = self.total(2, 1, 0).astype(BF)
-        return jnp.concatenate([rows0, rows1], axis=0)
+        return self.total(2, 1, 0).astype(BF).reshape(EXP * ROWS, HALF)
 
 
 def kernel(
@@ -243,33 +253,41 @@
     go = net.go
 
     class Exchange:
-        def __init__(self, rows, send_ref, arr_ref, via_ref, keep=None):
+        def __init__(self, send_ref, arr_ref, via_ref, keep=None):
+            self.send, self.arr, self.via, self.keep = send_ref, arr_ref, via_ref, keep
+            self.first, self.copies, self.own = {}, {}, []
+
+        def fill(self, rows, *units):
             for r in range(PLANES):
                 part = rows[r * SLAB : (r + 1) * SLAB].astype(BF)
-                if r == 0 and keep is None:
-                    arr_ref[0] = part
+                ref = self.arr if r == 0 and self.keep is None else self.send
+                if len(units) == 2:
+                    ref[r] = part
                 else:
-                    send_ref[r] = part
-            self.send, self.arr, self.via, self.keep = send_ref, arr_ref, via_ref, keep
-
-        def start(self):
-            lo, hi = pl.ds(0, HALF), pl.ds(HALF, HALF)
-            self.first = go(self.send.at[2, :, hi], self.via, zs[3])
-            self.copies = [go(self.send.at[2, :, lo], self.arr.at[2, :, lo], zs[2])]
-            self.copies += [go(self.send.at[r], self.arr.at[PLANES - r], zs[r]) for r in (3, 1)]
+                    ref[r, :, wide(units[0])] = part
+
+        def start(self, u):
+            lo, hi = pl.ds(u * HALF, HALF // 2), pl.ds(u * HALF + HALF // 2, HALF // 2)
+            self.first[u] = go(self.send.at[2, :, hi], self.via.at[u], zs[3])
+            self.copies[u] = [go(self.send.at[2, :, lo], self.arr.at[2, :, lo], zs[2])]
+            self.copies[u] += [go(self.send.at[r, :, wide(u)], self.arr.at[PLANES - r, :, wide(u)], zs[r]) for r in (3, 1)]
             if self.keep is not None:
-                self.own = pltpu.make_async_copy(self.send.at[0], self.arr.at[0], self.keep)
-                self.own.start()
-
-        def forward(self):
-            got(self.first)
-            self.copies.append(go(self.via, self.arr.at[2, :, pl.ds(HALF, HALF)], zs[3]))
-
-        def finish(self):
-            got(*self.copies)
-
-    ex = Exchange(dot(picks[0] + picks[1], tok[...]), send_x, arr_x, via.at[0])
-    ex.start()
+                own = pltpu.make_async_copy(self.send.at[0, :, wide(u)], self.arr.at[0, :, wide(u)], self.keep.at[u])
+                own.start()
+                self.own.append(own)
+
+        def forward(self, u):
+            got(self.first[u])
+            hi = pl.ds(u * HALF + HALF // 2, HALF // 2)
+            self.copies[u].append(go(self.via.at[u], self.arr.at[2, :, hi], zs[3]))
+
+        def finish(self, u):
+            got(*self.copies[u])
+
+    ex = Exchange(send_x, arr_x, via.at[0])
+    ex.fill(dot(picks[0] + picks[1], tok[...]), 0, 1)
+    ex.start(0)
+    ex.start(1)
 
     def weight(k, lo):
         return wgu.at[:, :, pl.ds(lo + k * FP, FP)]
@@ -282,24 +300,35 @@
 
     cotf = cot[...].astype(F32)
     rows_d = [(jnp.sum(jnp.where(row_t == col_t, gw[k : k + 1, :], 0.0), axis=1, keepdims=True) * cotf).astype(BF) for k in range(2)]
-    ed = Exchange(dot(picks[0], rows_d[0]) + dot(picks[1], rows_d[1]), send_d, arr_d, via.at[1])
-    ex.forward()
-
-    def chunk_in(arr_ref, g):
-        rows = dot(into, arr_ref[...].reshape(ALL, D)).astype(BF)
-        g[0, 0] = rows[:ROWS]
-        g[1, 0] = rows[ROWS:]
+    ed = Exchange(send_d, arr_d, via.at[1])
+    ed.fill(dot(picks[0], rows_d[0]) + dot(picks[1], rows_d[1]), 0, 1)
+
+    def chunk_in(arr_ref, g, u):
+        rows = dot(into, arr_ref[:, :, wide(u)].reshape(ALL, HALF)).astype(BF)
+        g[0, 0, :, wide(u)] = rows[:ROWS]
+        g[1, 0, :, wide(u)] = rows[ROWS:]
 
     gx, gd = Gather(net, xg, xp, yu, yd), Gather(net, dg, xp, yu, yd)
-    ex.finish()
-    chunk_in(arr_x, xg)
-    gx.start()
-    ed.start()
-    gx.step2()
-    ed.forward()
-    ed.finish()
-    chunk_in(arr_d, dg)
-    gd.start()
+    ex.forward(0)
+    ex.finish(0)
+    chunk_in(arr_x, xg, 0)
+    gx.start0()
+    ex.forward(1)
+    ex.finish(1)
+    chunk_in(arr_x, xg, 1)
+    gx.start1()
+    ed.start(0)
+    ed.start(1)
+    gx.step2a()
+    ed.forward(0)
+    ed.forward(1)
+    gx.step2b()
+    ed.finish(0)
+    ed.finish(1)
+    chunk_in(arr_d, dg, 0)
+    chunk_in(arr_d, dg, 1)
+    gd.start0()
+    gd.start1()
     got(cross[0])
     side.append(go(weight(1, 0), weight(3, 0), cp))
     gx.step3()
@@ -324,18 +353,18 @@
 
         lax.fori_loop(0, HID // 256, tile, 0)
 
-    def project(e):
-        def tile(n, _):
-            cols = pl.ds(pl.multiple_of(n * 256, 256), 256)
+    def project(u):
+        def tile(i, _):
+            e, cols = i // 2, pl.ds(pl.multiple_of(u * HALF + (i % 2) * 256, 256), 256)
             po[e, :, :, cols] = dot(hid[e], wdn[e, :, cols]).astype(BF).reshape(SLOTS, ROWS, 256)
             return 0
 
-        lax.fori_loop(0, D // 256, tile, 0)
-
-    gx.finish(0)
+        lax.fori_loop(0, 2 * EXP, tile, 0)
+
+    gx.finish()
     forward(0)
-    gd.step2()
-    gx.finish(1)
+    gd.step2a()
+    gd.step2b()
     forward(1)
     gd.step3()
     got(cross[2])
@@ -343,10 +372,10 @@
     got(late)
     ro = Reduce(net, po, near_o, far_o, across_o, xp, yu, yd)
     rv = Reduce(net, pv, near_v, far_v, across_v, xp, yu, yd)
+    project(1)
+    ro.start1()
     project(0)
     ro.start0()
-    project(1)
-    ro.start1()
 
     def backward(e):
         def tile(n, _):
@@ -358,14 +387,14 @@
 
         lax.fori_loop(0, HID // 256, tile, 0)
 
-    def propagate(e):
-        def tile(n, _):
-            cols = pl.ds(pl.multiple_of(n * 256, 256), 256)
+    def propagate(u):
+        def tile(i, _):
+            e, cols = i // 2, pl.ds(pl.multiple_of(u * HALF + (i % 2) * 256, 256), 256)
             part = dot(dgu[e], wgu[e, cols, :], (1, 1))
             pv[e, :, :, cols] = part.astype(BF).reshape(SLOTS, ROWS, 256)
             return 0
 
-        lax.fori_loop(0, D // 256, tile, 0)
+        lax.fori_loop(0, 2 * EXP, tile, 0)
 
     def down_grad(e):
         def tile(n, _):
@@ -414,40 +443,50 @@
             far.append(go(pgu.at[e, :, pl.ds(i * HID + FP, FP)], far_gu.at[i, e], xc))
             keep(pgu.at[e, :, pl.ds(i * HID, FP)], sum_gu.at[i, e])
 
-    gd.finish(0)
-    backward(0)
+    gd.finish()
     down_grad(0)
     share_down(0)
-    gd.finish(1)
-    backward(1)
-    ro.step2()
+    backward(0)
+    ro.step_a()
     down_grad(1)
     share_down(1)
     send_down(0)
+    backward(1)
+    send_down(1)
+    ro.step_b()
     up_grad(0)
     share_up(0)
-    send_down(1)
-    ro.step3()
-    up_grad(1)
-    share_up(1)
+    ro.step_c()
+    propagate(1)
+    rv.start1()
     send_up(0)
     propagate(0)
     rv.start0()
+    eo = Exchange(send_o, arr_o, via.at[2], local.at[pl.ds(9, 2)])
+    ev = Exchange(send_v, arr_v, via.at[3], local.at[pl.ds(11, 2)])
+    up_grad(1)
+    share_up(1)
+    eo.fill(dot(back, ro.final1()), 1)
+    eo.start(1)
+    eo.fill(dot(back, ro.final0()), 0)
+    eo.start(0)
     send_up(1)
-    propagate(1)
-    rv.start1()
-    eo = Exchange(dot(back, ro.step4()), send_o, arr_o, via.at[2], local.at[9])
-    eo.start()
-    rv.step2()
-    eo.forward()
-    rv.step3()
-    ev = Exchange(dot(back, rv.step4()), send_v, arr_v, via.at[3], local.at[10])
-    ev.start()
-    eo.finish()
-    ev.forward()
-    ev.finish()
+    rv.step_a()
+    eo.forward(1)
+    eo.forward(0)
+    rv.step_b()
+    rv.step_c()
+    ev.fill(dot(back, rv.final1()), 1)
+    ev.start(1)
+    ev.fill(dot(back, rv.final0()), 0)
+    ev.start(0)
+    ev.forward(1)
+    ev.forward(0)
+    for u in range(2):
+        eo.finish(u)
+        ev.finish(u)
     got(*far)
-    for copy in kept + [eo.own, ev.own]:
+    for copy in kept + eo.own + ev.own:
         copy.wait()
     for copy in net.all:
         copy.wait_send()
@@ -475,14 +514,14 @@
 
     slab = [buf(PLANES, SLAB, D) for _ in range(6)]
     big = [buf(EXP, SLOTS, ROWS, D) for _ in range(4)]
-    rings = [buf(3, 2, ROWS, HALF), buf(3, 2, ROWS, D), buf(5, ROWS, D)] * 2
-    scratch = slab + [buf(4, SLAB, HALF)] + big + rings + [
+    rings = [buf(3, 2, ROWS, HALF), buf(3, 2, EXP, ROWS, HALF), buf(5, EXP, ROWS, HALF)] * 2
+    scratch = slab + [buf(4, 2, SLAB, HALF // 2)] + big + rings + [
         buf(EXP, D, 2 * HID), buf(EXP, HID, D),
         buf(EXP, MINE, HID, dtype=F32), buf(EXP, MINE, HID, dtype=F32),
         buf(EXP, MINE, HID), buf(EXP, MINE, 2 * HID),
         buf(EXP, HID, D), buf(EXP, D, 2 * HID),
         buf(EXP, 2 * FP, D), buf(2, EXP, D, 2 * FP),
-        pltpu.SemaphoreType.DMA((COPIES,)), pltpu.SemaphoreType.DMA((COPIES,)), pltpu.SemaphoreType.DMA((11,)),
+        pltpu.SemaphoreType.DMA((COPIES,)), pltpu.SemaphoreType.DMA((COPIES,)), pltpu.SemaphoreType.DMA((13,)),
     ]
 
     def out(*shape):

time: 116 us -> 104 us (0.90)
  Pallas kernels: 115 us -> 104 us
    pallas_call x1, Pallas kernels: 110 us -> 99.6 us  [body(): pl.pallas_call(kernel, out_shape=(out(2, ALL, TOK), out(PLANES, SLAB, D),...]
where the time goes in v4:
time: 104 us
  Pallas kernels  104 us (100%)
    pallas_call x1, Pallas kernels, body(): pl.pallas_call(kernel, out_shape=(out(2, ALL, TOK), out(PLANES, SLAB, D),...  99.6 us
    pallas_call x1, Pallas kernels, body(): pl.pallas_call(finish, out_shape=tuple((jax.ShapeDtypeStruct(a.shape, BF)...  4.04 us

profile of v4, /device:TPU:1, one launch (start us, length us, event | category | flops | bytes accessed | tf_op | source)
XLA Modules:
  0.0 104.3 jit_solution(6967258336515521494)
XLA Ops:
  0.6 99.6 %shard_map.110 = (bf16[2,192,64]{2,1,0:T(8,128)(2,1)}, bf16[4,48,1024]{2,1,0:T(8,128)(2,1)}, bf16[4,48,1024]{2,1,0:T(8,128)(2,1)}, bf16[2,128,1024]{2,1,0:T(8,12...) custom-call(bf16[64,1024]{1,0:T(8,128)(2,1)} %tok.1, ...), custom_call_target="tpu_custom_call" | custom-call | tf_op jit(solution)/shard_map/pallas_call | solution.py:531
  100.3 4.0 %shard_map.111 = (bf16[64,1024]{1,0:T(8,128)(2,1)}, bf16[64,1024]{1,0:T(8,128)(2,1)}, bf16[2,1024,128]{2,1,0:T(8,128)(2,1)}, bf16[2,1024,128]{2,1,0:T(8,128)(2,1)}, bf16[2,128,1024]{2,1,0:T(8,128)(2,1)}) custom-call(f32[2,64]{1,0:T(2,128)} %bitcast.3, bf16[2,192,64]{2,1,0:T(8,128)(2,1)} %get-tuple-element.12.pick, ...), custom_call_target="tpu_custom_call" | custom-call | tf_op jit(solution)/shard_map/pallas_call | solution.py:544

commit v5 on v4

--- a/solution.py
+++ b/solution.py
@@ -184,11 +184,11 @@
 
 
 def kernel(
-    tok, ids, gw, cot, wg, wu, wd,
-    pick, arr_o, arr_v, sum_d, sum_gu, far_d, far_gu,
+    ids, gw, tok_in, cot_in, wg, wu, wd,
+    pick_out, arr_o, arr_v, sum_d, sum_gu, far_d, far_gu,
     send_x, send_d, send_o, send_v, arr_x, arr_d, via,
     xg, dg, po, pv, near_o, far_o, across_o, near_v, far_v, across_v,
-    wgu, wdn, fac_a, fac_b, hid, dgu, pd, pgu, rd, rgu,
+    tok, cot, pick, wgu, wdn, fac_a, fac_b, hid, dgu, pd, pgu, rd, rgu,
     send, recv, local,
 ):
     dp, z = lax.axis_index("dp"), lax.axis_index("expert")
@@ -207,12 +207,13 @@
     for device in (xp, xc, yu, yd, cp, zs[1], zs[2], zs[3]):
         pl.semaphore_signal(barrier, inc=1, device_id=device, device_id_type=MESH)
 
+    tokens_in = [pltpu.make_async_copy(tok_in, tok, local.at[13]), pltpu.make_async_copy(cot_in, cot, local.at[14])]
     own = [
         pltpu.make_async_copy(wg, wgu.at[:, :, pl.ds(0, FP)], local.at[0]),
         pltpu.make_async_copy(wu, wgu.at[:, :, pl.ds(HID, FP)], local.at[1]),
         pltpu.make_async_copy(wd, wdn.at[:, pl.ds(0, FP), :], local.at[2]),
     ]
-    for copy in own:
+    for copy in tokens_in + own:
         copy.start()
 
     expert = lax.broadcasted_iota(jnp.int32, (2 * PLANES, TOK), 0)
@@ -232,24 +233,7 @@
         picks.append(jnp.where(slab_row == base.astype(F32) + place, 1.0, 0.0).astype(BF))
         pick[k] = picks[k]
 
-    def from_slab(c):
-        s = (c >= SLAB).astype(jnp.int32) + (c >= 2 * SLAB).astype(jnp.int32) + (c >= 3 * SLAB).astype(jnp.int32)
-        rest = c - SLAB * s
-        j = (rest >= CAP).astype(jnp.int32)
-        row = j * ROWS + s * CAP + rest - CAP * j
-        return jnp.where(rest < EXP * CAP, row, -1)
-
-    into = jnp.where(
-        from_slab(lax.broadcasted_iota(jnp.int32, (EXP * ROWS, ALL), 1))
-        == lax.broadcasted_iota(jnp.int32, (EXP * ROWS, ALL), 0), 1.0, 0.0,
-    ).astype(BF)
-    back = jnp.where(
-        from_slab(lax.broadcasted_iota(jnp.int32, (ALL, EXP * ROWS), 0))
-        == lax.broadcasted_iota(jnp.int32, (ALL, EXP * ROWS), 1), 1.0, 0.0,
-    ).astype(BF)
-
     net = Net(send, recv)
-    pl.semaphore_wait(barrier, 8)
     go = net.go
 
     class Exchange:
@@ -285,7 +269,9 @@
             got(*self.copies[u])
 
     ex = Exchange(send_x, arr_x, via.at[0])
+    tokens_in[0].wait()
     ex.fill(dot(picks[0] + picks[1], tok[...]), 0, 1)
+    pl.semaphore_wait(barrier, 8)
     ex.start(0)
     ex.start(1)
 
@@ -298,10 +284,27 @@
     cross = [go(wg, weight(1, 0), xc), go(wu, weight(1, HID), xc), go(wd, down(1), xc)]
     side = [go(wg, weight(2, 0), cp), go(wu, weight(2, HID), cp), go(wd, down(2), cp)]
 
+    tokens_in[1].wait()
     cotf = cot[...].astype(F32)
     rows_d = [(jnp.sum(jnp.where(row_t == col_t, gw[k : k + 1, :], 0.0), axis=1, keepdims=True) * cotf).astype(BF) for k in range(2)]
     ed = Exchange(send_d, arr_d, via.at[1])
     ed.fill(dot(picks[0], rows_d[0]) + dot(picks[1], rows_d[1]), 0, 1)
+
+    def from_slab(c):
+        s = (c >= SLAB).astype(jnp.int32) + (c >= 2 * SLAB).astype(jnp.int32) + (c >= 3 * SLAB).astype(jnp.int32)
+        rest = c - SLAB * s
+        j = (rest >= CAP).astype(jnp.int32)
+        row = j * ROWS + s * CAP + rest - CAP * j
+        return jnp.where(rest < EXP * CAP, row, -1)
+
+    into = jnp.where(
+        from_slab(lax.broadcasted_iota(jnp.int32, (EXP * ROWS, ALL), 1))
+        == lax.broadcasted_iota(jnp.int32, (EXP * ROWS, ALL), 0), 1.0, 0.0,
+    ).astype(BF)
+    back = jnp.where(
+        from_slab(lax.broadcasted_iota(jnp.int32, (ALL, EXP * ROWS), 0))
+        == lax.broadcasted_iota(jnp.int32, (ALL, EXP * ROWS), 1), 1.0, 0.0,
+    ).astype(BF)
 
     def chunk_in(arr_ref, g, u):
         rows = dot(into, arr_ref[:, :, wide(u)].reshape(ALL, HALF)).astype(BF)
@@ -443,6 +446,8 @@
             far.append(go(pgu.at[e, :, pl.ds(i * HID + FP, FP)], far_gu.at[i, e], xc))
             keep(pgu.at[e, :, pl.ds(i * HID, FP)], sum_gu.at[i, e])
 
+    picks_out = pltpu.make_async_copy(pick, pick_out, local.at[15])
+    picks_out.start()
     gd.finish()
     down_grad(0)
     share_down(0)
@@ -486,7 +491,7 @@
         eo.finish(u)
         ev.finish(u)
     got(*far)
-    for copy in kept + eo.own + ev.own:
+    for copy in kept + eo.own + ev.own + [picks_out]:
         copy.wait()
     for copy in net.all:
         copy.wait_send()
@@ -516,12 +521,13 @@
     big = [buf(EXP, SLOTS, ROWS, D) for _ in range(4)]
     rings = [buf(3, 2, ROWS, HALF), buf(3, 2, EXP, ROWS, HALF), buf(5, EXP, ROWS, HALF)] * 2
     scratch = slab + [buf(4, 2, SLAB, HALF // 2)] + big + rings + [
+        buf(TOK, D), buf(TOK, D), buf(2, ALL, TOK),
         buf(EXP, D, 2 * HID), buf(EXP, HID, D),
         buf(EXP, MINE, HID, dtype=F32), buf(EXP, MINE, HID, dtype=F32),
         buf(EXP, MINE, HID), buf(EXP, MINE, 2 * HID),
         buf(EXP, HID, D), buf(EXP, D, 2 * HID),
         buf(EXP, 2 * FP, D), buf(2, EXP, D, 2 * FP),
-        pltpu.SemaphoreType.DMA((COPIES,)), pltpu.SemaphoreType.DMA((COPIES,)), pltpu.SemaphoreType.DMA((13,)),
+        pltpu.SemaphoreType.DMA((COPIES,)), pltpu.SemaphoreType.DMA((COPIES,)), pltpu.SemaphoreType.DMA((16,)),
     ]
 
     def out(*shape):
@@ -534,13 +540,13 @@
             out(2, ALL, TOK), out(PLANES, SLAB, D), out(PLANES, SLAB, D),
             out(EXP, FP, D), out(2, EXP, D, FP), out(EXP, FP, D), out(2, EXP, D, FP),
         ),
-        in_specs=[vmem] * 4 + [hbm] * 3,
-        out_specs=(vmem,) + (hbm,) * 6,
+        in_specs=[vmem] * 2 + [hbm] * 5,
+        out_specs=(hbm,) * 7,
         scratch_shapes=scratch,
         compiler_params=pltpu.CompilerParams(
             collective_id=0, has_side_effects=True, vmem_limit_bytes=67043328
         ),
-    )(tokens, expert_ids.T, weights, cotangent, w_gate, w_up, w_down)
+    )(expert_ids.T, weights, tokens, cotangent, w_gate, w_up, w_down)
     return pl.pallas_call(
         finish,
         out_shape=tuple(

time: 104 us -> 103 us (level)
    pallas_call x1, Pallas kernels: 99.6 us -> 98.5 us  [body(): pl.pallas_call(kernel, out_shape=(out(2, ALL, TOK), out(PLANES, SLAB, D),...]
where the time goes in v5:
time: 103 us
  Pallas kernels  103 us (100%)
    pallas_call x1, Pallas kernels, body(): pl.pallas_call(kernel, out_shape=(out(2, ALL, TOK), out(PLANES, SLAB, D),...  98.5 us
    pallas_call x1, Pallas kernels, body(): pl.pallas_call(finish, out_shape=tuple((jax.ShapeDtypeStruct(a.shape, BF)...  4.04 us

profile of v5, /device:TPU:1, one launch (start us, length us, event | category | flops | bytes accessed | tf_op | source)
XLA Modules:
  0.0 103.1 jit_solution(130208026718873779)
XLA Ops:
  0.6 98.5 %shard_map.110 = (bf16[2,192,64]{2,1,0:T(8,128)(2,1)}, bf16[4,48,1024]{2,1,0:T(8,128)(2,1)}, bf16[4,48,1024]{2,1,0:T(8,128)(2,1)}, bf16[2,128,1024]{2,1,0:T(8,12...) custom-call(s32[2,64]{1,0:T(2,128)} %bitcast.4, ...), custom_call_target="tpu_custom_call" | custom-call | tf_op jit(solution)/shard_map/pallas_call | solution.py:537
  99.1 4.0 %shard_map.111 = (bf16[64,1024]{1,0:T(8,128)(2,1)}, bf16[64,1024]{1,0:T(8,128)(2,1)}, bf16[2,1024,128]{2,1,0:T(8,128)(2,1)}, bf16[2,1024,128]{2,1,0:T(8,128)(2,1)}, bf16[2,128,1024]{2,1,0:T(8,128)(2,1)}) custom-call(f32[2,64]{1,0:T(2,128)} %bitcast.3, bf16[2,192,64]{2,1,0:T(8,128)(2,1)} %get-tuple-element.12.pick, ...), custom_call_target="tpu_custom_call" | custom-call | tf_op jit(solution)/shard_map/pallas_call | solution.py:550

commit v6 on v5

--- a/solution.py
+++ b/solution.py
@@ -169,6 +169,8 @@
     def step_c(self):
         self.p[:, 4, :, wide(0)] = self.total(1, 0, 4).astype(BF)
         self.x0 = self.net.go(full(self.p, 0, 4), self.across.at[4], self.xp)
+
+    def step_d(self):
         self.joined(3)
         self.free_down(2, 1, 0)
         self.inner(2, 1, 0)
@@ -464,6 +466,7 @@
     ro.step_c()
     propagate(1)
     rv.start1()
+    ro.step_d()
     send_up(0)
     propagate(0)
     rv.start0()
@@ -480,6 +483,7 @@
     eo.forward(1)
     eo.forward(0)
     rv.step_b()
+    rv.step_d()
     rv.step_c()
     ev.fill(dot(back, rv.final1()), 1)
     ev.start(1)

time: 103 us -> 103 us (level)
  no operation moved by 1% of the time
where the time goes in v6:
time: 103 us
  Pallas kernels  102 us (99%)
    pallas_call x1, Pallas kernels, body(): pl.pallas_call(kernel, out_shape=(out(2, ALL, TOK), out(PLANES, SLAB, D),...  98.5 us
    pallas_call x1, Pallas kernels, body(): pl.pallas_call(finish, out_shape=tuple((jax.ShapeDtypeStruct(a.shape, BF)...  4.04 us

profile of v6, /device:TPU:1, one launch (start us, length us, event | category | flops | bytes accessed | tf_op | source)
XLA Modules:
  0.0 103.1 jit_solution(4304006845137226222)
XLA Ops:
  0.6 98.5 %shard_map.110 = (bf16[2,192,64]{2,1,0:T(8,128)(2,1)}, bf16[4,48,1024]{2,1,0:T(8,128)(2,1)}, bf16[4,48,1024]{2,1,0:T(8,128)(2,1)}, bf16[2,128,1024]{2,1,0:T(8,12...) custom-call(s32[2,64]{1,0:T(2,128)} %bitcast.4, ...), custom_call_target="tpu_custom_call" | custom-call | tf_op jit(solution)/shard_map/pallas_call | solution.py:541
  99.1 4.0 %shard_map.111 = (bf16[64,1024]{1,0:T(8,128)(2,1)}, bf16[64,1024]{1,0:T(8,128)(2,1)}, bf16[2,1024,128]{2,1,0:T(8,128)(2,1)}, bf16[2,1024,128]{2,1,0:T(8,128)(2,1)}, bf16[2,128,1024]{2,1,0:T(8,128)(2,1)}) custom-call(f32[2,64]{1,0:T(2,128)} %bitcast.3, bf16[2,192,64]{2,1,0:T(8,128)(2,1)} %get-tuple-element.12.pick, ...), custom_call_target="tpu_custom_call" | custom-call | tf_op jit(solution)/shard_map/pallas_call | solution.py:554
